TPU v7x, 32 devices: a whole 2x2x4 slice. The times are simulated.
32 devices in a mesh: tile: 16 (over z, x, core), mem: 2 (over y).
Axes of the slice: x: 2, y: 2, z: 4, core: 2. Of those that a mesh axis runs over, the one named last changes fastest.
Arguments:
- ensemble: float32 [64, 7, 32768], P('mem', None, 'tile'), may hold values from -6 to 6
- obs_site: int32 [8, 32], replicated, may hold values from 0 to 14335
- obs_value: float32 [8, 32], replicated, may hold values from -8 to 8
- obs_var: float32 [8, 32], replicated, may hold values from 4 to 32
- owner_tile: int32 [8], replicated, may hold values from 0 to 15
- tile_mask: int32 [8, 16], replicated, may hold values 0 or 1
- batch_order: int32 [8], replicated, may hold values from 0 to 7, each once
Outputs:
- posterior: float32 [64, 7, 32768], P('mem', None, 'tile')
All inputs are finite; a program needn't handle non-finite values.
Results may differ from a plain program's by a relative error of at most 0.0001.
Values sent between devices are 32-bit elements; how exact they have to be, the bound alone decides.
No kernel may reach another device: no remote copies, remote signals or barrier semaphores. Data moves between devices by JAX's collectives and lax.ppermute only.
A program may use at most 64 MiB of HBM per device.

v0:
```python
import jax
import jax.numpy as jnp
from jax import lax
from jax.sharding import PartitionSpec as P

BATCHES = 8


def from_root(block, axis, holder):
    block = jnp.where(lax.axis_index(axis) == holder, block, jnp.zeros_like(block))
    return lax.psum(block, axis)


def batch_transform(priors, values, variances):
    count = priors.shape[1]
    highest = lax.Precision.HIGHEST

    def assimilate(transform, inputs):
        prior_row, value, variance = inputs
        y_row = jnp.dot(prior_row, transform, precision=highest)
        ens_mean = jnp.mean(y_row)
        spread = y_row - ens_mean
        sample_var = jnp.sum(spread * spread) / (count - 1)
        inv_total = 1.0 / (sample_var + variance)
        alpha = 1.0 / (1.0 + jnp.sqrt(variance * inv_total))
        weights = inv_total / (count - 1) * (value - ens_mean - alpha * spread)
        moved = jnp.dot(transform, spread, precision=highest)
        return (transform + moved[:, None] * weights[None, :], None)

    start_eye = jnp.eye(count, dtype=jnp.float32)
    result, _ = lax.scan(assimilate, start_eye, (priors, values, variances))
    return result


def body(ensemble, obs_site, obs_value, obs_var, owner_tile, tile_mask, batch_order):
    highest = lax.Precision.HIGHEST
    local_members = ensemble.shape[0]
    all_members = local_members * lax.axis_size("mem")
    tile_idx = lax.axis_index("tile")
    mem_idx = lax.axis_index("mem")
    flat_state = ensemble.reshape(local_members, -1)
    combined = jnp.eye(all_members, dtype=jnp.float32)
    for position in range(BATCHES):
        batch_id = batch_order[position]
        local_rows = jnp.take(flat_state, obs_site[batch_id], axis=1)
        obs_rows = lax.all_gather(local_rows, "mem", axis=0, tiled=True)
        own_priors = jnp.dot(obs_rows.T, combined, precision=highest)
        priors = from_root(own_priors, "tile", owner_tile[batch_id])
        transform = batch_transform(priors, obs_value[batch_id], obs_var[batch_id])
        updated = jnp.dot(combined, transform, precision=highest)
        combined = jnp.where(
            (tile_mask[batch_id, tile_idx] == 1) | (owner_tile[batch_id] == tile_idx),
            updated,
            combined,
        )
    my_columns = lax.dynamic_slice_in_dim(combined, mem_idx * local_members, local_members, 1)
    return jnp.einsum(
        "mn,mvc->nvc",
        my_columns,
        lax.all_gather(ensemble, "mem", axis=0, tiled=True),
        precision=highest,
    )


def solution(mesh):
    return jax.shard_map(
        body,
        mesh=mesh,
        in_specs=(P("mem", None, "tile"), P(), P(), P(), P(), P(), P()),
        out_specs=P("mem", None, "tile"),
        check_vma=False,
    )
```

profile of v0, /device:TPU:0, one launch (start us, length us, event | category | flops | bytes accessed | tf_op | source)
XLA Modules:
  0.0 2158.5 jit_solution(17621511112711468717)
XLA Ops:
  7.3 1.6 fusion.73
  18.7 6.0 copy.17
  39.2 3.7 gather_fusion
  43.0 5.8 all_gather.27
  49.0 61.2 %psum.56 = f32[32,64]{1,0:T(8,128)S(1)} all-reduce(f32[32,64]{1,0:T(8,128)S(1)} %convolution_select_fusion.14), channel_id=1, replica_groups=mesh['tile'=16,'mem'=2] {'tile'}, use_global_device_ids=true, to_apply=%region_0.0 | all-reduce | flops 2048 | bytes 16384 | tf_op jit(solution)/shard_map/psum | solution.py:11
  110.2 211.1 %while.80 = (s32[]{:T(128)}, f32[64,64]{1,0:T(8,128)S(1)}, f32[32,64]{1,0:T(8,128)S(1)}, f32[32]{0:T(128)S(1)}, f32[32]{0:T(128)S(1)}, /*index=5*/s32[]{:T(128)}, f32[]{:T(128)}, f32[]{:T(128)}, f32[]{:T(128)}) while((s32[]{:T(128)}, f32[64,64]{1,0:T(8,128)S(1)}, f32[32,64]{1,0:T(8,128)S(1)}, f32[32]{0:T(128)S(1)}, f32[32]{0:T(128)S(1)}, ...), condition=%wide.region_4.6_spmd, body=%wide.region_1.0_spmd.sunk | while | flops 107081 | bytes 84749 | solution.py:31
  321.3 3.7 gather_fusion.1
  325.2 4.4 all_gather.28
  331.3 57.6 %psum.57 = f32[32,64]{1,0:T(8,128)S(1)} all-reduce(f32[32,64]{1,0:T(8,128)S(1)} %convolution_select_fusion.13), channel_id=1, replica_groups=mesh['tile'=16,'mem'=2] {'tile'}, use_global_device_ids=true, to_apply=%region_5.7 | all-reduce | flops 2048 | bytes 16384 | tf_op jit(solution)/shard_map/psum | solution.py:11
  388.9 195.8 %while.81 = (s32[]{:T(128)}, f32[64,64]{1,0:T(8,128)S(1)}, f32[32,64]{1,0:T(8,128)S(1)}, f32[32]{0:T(128)S(1)}, f32[32]{0:T(128)S(1)}, /*index=5*/s32[]{:T(128)}, f32[]{:T(128)}, f32[]{:T(128)}, f32[]{:T(128)}) while((s32[]{:T(128)}, f32[64,64]{1,0:T(8,128)S(1)}, f32[32,64]{1,0:T(8,128)S(1)}, f32[32]{0:T(128)S(1)}, f32[32]{0:T(128)S(1)}, ...), condition=%wide.region_9.11_spmd, body=%wide.region_6.10_spmd.sunk | while | flops 107081 | bytes 84749 | solution.py:31
  585.4 3.7 gather_fusion.2
  589.2 4.4 all_gather.29
  594.1 57.6 %psum.58 = f32[32,64]{1,0:T(8,128)S(1)} all-reduce(f32[32,64]{1,0:T(8,128)S(1)} %convolution_select_fusion.12), channel_id=1, replica_groups=mesh['tile'=16,'mem'=2] {'tile'}, use_global_device_ids=true, to_apply=%region_10.12 | all-reduce | flops 2048 | bytes 16384 | tf_op jit(solution)/shard_map/psum | solution.py:11
  651.7 183.3 %while.82 = (s32[]{:T(128)}, f32[64,64]{1,0:T(8,128)S(1)}, f32[32,64]{1,0:T(8,128)S(1)}, f32[32]{0:T(128)S(1)}, f32[32]{0:T(128)S(1)}, /*index=5*/s32[]{:T(128)}, f32[]{:T(128)}, f32[]{:T(128)}, f32[]{:T(128)}) while((s32[]{:T(128)}, f32[64,64]{1,0:T(8,128)S(1)}, f32[32,64]{1,0:T(8,128)S(1)}, f32[32]{0:T(128)S(1)}, f32[32]{0:T(128)S(1)}, ...), condition=%wide.region_14.16_spmd, body=%wide.region_11.15_spmd.sunk | while | flops 107081 | bytes 84749 | solution.py:31
  835.7 3.7 gather_fusion.3
  839.5 4.4 all_gather.30
  844.4 57.6 %psum.59 = f32[32,64]{1,0:T(8,128)S(1)} all-reduce(f32[32,64]{1,0:T(8,128)S(1)} %convolution_select_fusion.11), channel_id=1, replica_groups=mesh['tile'=16,'mem'=2] {'tile'}, use_global_device_ids=true, to_apply=%region_15.17 | all-reduce | flops 2048 | bytes 16384 | tf_op jit(solution)/shard_map/psum | solution.py:11
  902.0 185.8 %while.83 = (s32[]{:T(128)}, f32[64,64]{1,0:T(8,128)S(1)}, f32[32,64]{1,0:T(8,128)S(1)}, f32[32]{0:T(128)S(1)}, f32[32]{0:T(128)S(1)}, /*index=5*/s32[]{:T(128)}, f32[]{:T(128)}, f32[]{:T(128)}, f32[]{:T(128)}) while((s32[]{:T(128)}, f32[64,64]{1,0:T(8,128)S(1)}, f32[32,64]{1,0:T(8,128)S(1)}, f32[32]{0:T(128)S(1)}, f32[32]{0:T(128)S(1)}, ...), condition=%wide.region_19.21_spmd, body=%wide.region_16.20_spmd.sunk | while | flops 107081 | bytes 84749 | solution.py:31
  1088.5 3.7 gather_fusion.4
  1092.3 4.4 all_gather.31
  1097.2 57.6 %psum.60 = f32[32,64]{1,0:T(8,128)S(1)} all-reduce(f32[32,64]{1,0:T(8,128)S(1)} %convolution_select_fusion.10), channel_id=1, replica_groups=mesh['tile'=16,'mem'=2] {'tile'}, use_global_device_ids=true, to_apply=%region_20.22 | all-reduce | flops 2048 | bytes 16384 | tf_op jit(solution)/shard_map/psum | solution.py:11
  1154.8 194.4 %while.84 = (s32[]{:T(128)}, f32[64,64]{1,0:T(8,128)S(1)}, f32[32,64]{1,0:T(8,128)S(1)}, f32[32]{0:T(128)S(1)}, f32[32]{0:T(128)S(1)}, /*index=5*/s32[]{:T(128)}, f32[]{:T(128)}, f32[]{:T(128)}, f32[]{:T(128)}) while((s32[]{:T(128)}, f32[64,64]{1,0:T(8,128)S(1)}, f32[32,64]{1,0:T(8,128)S(1)}, f32[32]{0:T(128)S(1)}, f32[32]{0:T(128)S(1)}, ...), condition=%wide.region_24.26_spmd, body=%wide.region_21.25_spmd.sunk | while | flops 107081 | bytes 84749 | solution.py:31
  1349.9 3.7 gather_fusion.5
  1353.7 4.4 all_gather.32
  1358.6 57.6 %psum.61 = f32[32,64]{1,0:T(8,128)S(1)} all-reduce(f32[32,64]{1,0:T(8,128)S(1)} %convolution_select_fusion.9), channel_id=1, replica_groups=mesh['tile'=16,'mem'=2] {'tile'}, use_global_device_ids=true, to_apply=%region_25.27 | all-reduce | flops 2048 | bytes 16384 | tf_op jit(solution)/shard_map/psum | solution.py:11
  1416.2 184.1 %while.85 = (s32[]{:T(128)}, f32[64,64]{1,0:T(8,128)S(1)}, f32[32,64]{1,0:T(8,128)S(1)}, f32[32]{0:T(128)S(1)}, f32[32]{0:T(128)S(1)}, /*index=5*/s32[]{:T(128)}, f32[]{:T(128)}, f32[]{:T(128)}, f32[]{:T(128)}) while((s32[]{:T(128)}, f32[64,64]{1,0:T(8,128)S(1)}, f32[32,64]{1,0:T(8,128)S(1)}, f32[32]{0:T(128)S(1)}, f32[32]{0:T(128)S(1)}, ...), condition=%wide.region_29.31_spmd, body=%wide.region_26.30_spmd.sunk | while | flops 107081 | bytes 84749 | solution.py:31
  1601.0 3.7 gather_fusion.6
  1604.8 4.4 all_gather.33
  1609.6 57.6 %psum.62 = f32[32,64]{1,0:T(8,128)S(1)} all-reduce(f32[32,64]{1,0:T(8,128)S(1)} %convolution_select_fusion.8), channel_id=1, replica_groups=mesh['tile'=16,'mem'=2] {'tile'}, use_global_device_ids=true, to_apply=%region_30.32 | all-reduce | flops 2048 | bytes 16384 | tf_op jit(solution)/shard_map/psum | solution.py:11
  1667.3 195.4 %while.86 = (s32[]{:T(128)}, f32[64,64]{1,0:T(8,128)S(1)}, f32[32,64]{1,0:T(8,128)S(1)}, f32[32]{0:T(128)S(1)}, f32[32]{0:T(128)S(1)}, /*index=5*/s32[]{:T(128)}, f32[]{:T(128)}, f32[]{:T(128)}, f32[]{:T(128)}) while((s32[]{:T(128)}, f32[64,64]{1,0:T(8,128)S(1)}, f32[32,64]{1,0:T(8,128)S(1)}, f32[32]{0:T(128)S(1)}, f32[32]{0:T(128)S(1)}, ...), condition=%wide.region_34.36_spmd, body=%wide.region_31.35_spmd.sunk | while | flops 107081 | bytes 84749 | solution.py:31
  1863.4 3.7 gather_fusion.7
  1867.2 4.4 all_gather.34
  1872.7 57.6 %psum.63 = f32[32,64]{1,0:T(8,128)S(1)} all-reduce(f32[32,64]{1,0:T(8,128)S(1)} %convolution_select_fusion.7), channel_id=1, replica_groups=mesh['tile'=16,'mem'=2] {'tile'}, use_global_device_ids=true, to_apply=%region_35.37 | all-reduce | flops 2048 | bytes 16384 | tf_op jit(solution)/shard_map/psum | solution.py:11
  1930.3 214.7 %while.87 = (s32[]{:T(128)}, f32[64,64]{1,0:T(8,128)S(1)}, f32[32,64]{1,0:T(8,128)S(1)}, f32[32]{0:T(128)S(1)}, f32[32]{0:T(128)S(1)}, /*index=5*/s32[]{:T(128)}, f32[]{:T(128)}, f32[]{:T(128)}, f32[]{:T(128)}) while((s32[]{:T(128)}, f32[64,64]{1,0:T(8,128)S(1)}, f32[32,64]{1,0:T(8,128)S(1)}, f32[32]{0:T(128)S(1)}, f32[32]{0:T(128)S(1)}, ...), condition=%wide.region_39.41_spmd, body=%wide.region_36.40_spmd.sunk | while | flops 107081 | bytes 84749 | solution.py:31
  1937.0 0.9 fusion.185
  1943.7 0.9 fusion.185
  1950.4 0.9 fusion.185
  1957.1 0.9 fusion.185
  1963.8 0.9 fusion.185
  1970.5 0.9 fusion.185
  1983.9 0.9 fusion.185
  2004.1 0.9 fusion.185
  2024.2 0.9 fusion.185
  2057.8 0.9 fusion.185
  2077.9 0.9 fusion.185
  2111.4 0.9 fusion.185
  2131.6 0.9 fusion.185
  2146.5 5.1 fusion.34
  (1845 shorter events, 738.1 us)
Async XLA Ops:
  6.5 23.1 %copy-start = (s32[8]{0:T(128)S(1)}, s32[8]{0:T(128)}, u32[]{:S(2)}) copy-start(s32[8]{0:T(128)} %param.29) | copy-start | bytes 100
  6.5 32.6 %copy-start.4 = (s32[8,32]{1,0:T(8,128)S(1)}, s32[8,32]{1,0:T(8,128)}, u32[]{:S(2)}) copy-start(s32[8,32]{1,0:T(8,128)} %param.26) | copy-start | bytes 3076
  6.5 103.7 %copy-start.2 = (f32[8,32]{1,0:T(8,128)S(1)}, f32[8,32]{1,0:T(8,128)}, u32[]{:S(2)}) copy-start(f32[8,32]{1,0:T(8,128)} %param.27) | copy-start | bytes 3076
  6.5 103.7 %copy-start.1 = (f32[8,32]{1,0:T(8,128)S(1)}, f32[8,32]{1,0:T(8,128)}, u32[]{:S(2)}) copy-start(f32[8,32]{1,0:T(8,128)} %param.28) | copy-start | bytes 3076
  6.5 323.0 %copy-start.3 = (s32[8,16]{1,0:T(8,128)S(1)}, s32[8,16]{1,0:T(8,128)}, u32[]{:S(2)}) copy-start(s32[8,16]{1,0:T(8,128)} %param.30) | copy-start | bytes 1540
  6.5 2140.0 %all-gather.2.cloned.1.call-start = ((), (), s32[]{:S(2)}) async-start(), calls=%async_computation | async-start | bytes 5505024 | tf_op jit(solution)/shard_map/all_gather | solution.py:60
Sparse Core Ops, SparseCore 0:
  8.9 53.8 all-gather.1
where the time goes:
time: 2170 us; the launch traced here: 2160 us
  loops' own time  822 us (38%)
  blocking collectives  501 us (23%)
  local copies, waits for them, and re-layouts  355 us (16%)
  matrix products  251 us (12%)
  other arithmetic  184 us (8%)
  between operations  43.6 us (2%)
    another operation x8, loops' own time, batch_transform(): result, _ = lax.scan(assimilate, start_eye, (priors, values, variances))  822 us
    psum x8, blocking collectives, from_root(): return lax.psum(block, axis)  465 us
    dynamic_slice x512, local copies, waits for them, and re-layouts, batch_transform(): result, _ = lax.scan(assimilate, start_eye, (priors, values, variances))  316 us
    dot_general x256, matrix products, assimilate(): y_row = jnp.dot(prior_row, transform, precision=highest)  207 us
    reduce_sum x256, other arithmetic, assimilate(): sample_var = jnp.sum(spread * spread) / (count - 1)  161 us
  transfers between devices with their start and end apart: 1, of which 0 were waited for; matrix products, arithmetic and copies ran while one was open for 36% of the time, Pallas kernels for 0%

commit v1 on v0

v1 whole, which is shorter than its diff:
```python
import functools

import jax
import jax.numpy as jnp
from jax import lax
from jax.experimental import pallas as pl
from jax.experimental.pallas import tpu as pltpu
from jax.sharding import PartitionSpec as P

LANES = 128
SUBS = 8
SMEM = pl.BlockSpec(memory_space=pltpu.SMEM)
VMEM = pl.BlockSpec(memory_space=pltpu.VMEM)


def gather_kernel(site_ref, owner_ref, order_ref, tile_ref, ens_ref, out_ref):
    batches, obs = site_ref.shape
    cells = ens_ref.shape[2]
    members = ens_ref.shape[1]
    per = LANES // obs
    lane = lax.broadcasted_iota(jnp.int32, (members, LANES), 1)
    out_ref[...] = jnp.zeros_like(out_ref)

    def one(p, carry):
        b = order_ref[p]

        @pl.when(owner_ref[b] == tile_ref[0])
        def _():
            base = lax.rem(p, per) * obs
            spot = pl.ds(pl.multiple_of(lax.div(p, per) * LANES, LANES), LANES)
            acc = out_ref[:, spot]
            for k in range(obs):
                site = site_ref[b, k]
                chan = lax.div(site, cells)
                cell = site - chan * cells
                col = lax.rem(cell, LANES)
                start = pl.multiple_of(cell - col, LANES)
                block = ens_ref[chan, :, pl.ds(start, LANES)]
                at = base + k
                turned = pltpu.roll(block, lax.rem(at - col + LANES, LANES), 1)
                acc = jnp.where(lane == at, turned, acc)
            out_ref[:, spot] = acc

        return carry

    lax.fori_loop(0, batches, one, 0)


def gather_rows(ens, obs_site, owner_tile, batch_order, tile):
    batches, obs = obs_site.shape
    return pl.pallas_call(
        gather_kernel,
        out_shape=jax.ShapeDtypeStruct((ens.shape[1], batches * obs), jnp.float32),
        in_specs=[SMEM, SMEM, SMEM, SMEM, VMEM],
        out_specs=VMEM,
        name="gather_rows",
    )(obs_site, owner_tile, batch_order, tile, ens)


def spread(row):
    return jnp.broadcast_to(row, (SUBS, row.shape[1]))


def chain_kernel(order_ref, owner_ref, mask_ref, var_ref, tile_ref, own_ref, oth_ref, val_ref,
                 out_ref, w_ref, left_ref, right_ref, z_ref, v_ref, val_s):
    batches, obs = val_ref.shape
    half = own_ref.shape[0]
    members = 2 * half
    total = batches * obs
    tiles = total // LANES
    per = LANES // obs
    blocks = obs // SUBS
    width = w_ref.shape[0]
    inv = 1.0 / (members - 1)
    highest = lax.Precision.HIGHEST
    contract = functools.partial(
        lax.dot_general, dimension_numbers=(((0,), (0,)), ((), ())), precision=highest,
        preferred_element_type=jnp.float32)
    lane1 = lax.broadcasted_iota(jnp.int32, (1, LANES), 1)
    lane8 = lax.broadcasted_iota(jnp.int32, (SUBS, LANES), 1)
    sub8 = lax.broadcasted_iota(jnp.int32, (SUBS, LANES), 0)
    tile = tile_ref[0]

    val_s[...] = jnp.zeros_like(val_s)
    val_s[:, :obs] = val_ref[...]
    values = []
    for t in range(tiles):
        row = jnp.zeros((1, LANES), jnp.float32)
        for q in range(per):
            one = val_s[pl.ds(order_ref[t * per + q], 1), :]
            row = row + (pltpu.roll(one, q * obs, 1) if q else one)
        values.append(row)
    values = jnp.concatenate(values, axis=1)

    raw = jnp.concatenate([own_ref[...], oth_ref[...]], axis=0)
    mean = jnp.sum(raw, axis=0, keepdims=True) * (1.0 / members)
    anom = raw - mean
    first = lax.broadcasted_iota(jnp.int32, (SUBS, total), 0) == 0
    lhs = jnp.concatenate([anom, jnp.where(first, values - mean, 0.0)], axis=0)
    depth = members + SUBS
    r_i = lax.broadcasted_iota(jnp.int32, (depth, 2 * LANES), 0)
    l_i = lax.broadcasted_iota(jnp.int32, (depth, 2 * LANES), 1)
    pick = jnp.where((r_i < members) & ((l_i == r_i) | (l_i == r_i + members)), 1.0, 0.0)
    pick = jnp.where((r_i == members) & (l_i == LANES), 1.0, pick)
    rhs = jnp.concatenate(
        [jnp.concatenate([anom, jnp.zeros((SUBS, total), jnp.float32)], axis=0), pick], axis=1)
    full = contract(lhs, rhs)
    for t in range(width):
        w_ref[t] = full[:, t * LANES:(t + 1) * LANES]

    def batch(p, carry):
        b = order_ref[p]
        o = owner_ref[b]
        mine = (mask_ref[b, tile] == 1) | (o == tile)
        mine_f = jnp.where(mine, 1.0, 0.0)
        act = []
        late = []
        for t in range(tiles):
            row = jnp.zeros((1, LANES), jnp.float32)
            row_late = jnp.zeros((1, LANES), jnp.float32)
            for q in range(per):
                other = owner_ref[order_ref[t * per + q]]
                on = (mask_ref[b, other] == 1) | (o == other)
                here = (lane1 >= q * obs) & (lane1 < (q + 1) * obs)
                row = jnp.where(here, jnp.where(on, 1.0, 0.0), row)
                row_late = jnp.where(here, jnp.where(t * per + q > p, 1.0, 0.0), row_late)
            act.append(row)
            late.append(row_late)
        act8 = [spread(a) > 0.5 for a in act]
        z_on = jnp.where(lane8 < members, mine_f, 0.0) > 0.5
        pick_w = act8 + [z_on, lane8 == 0]
        pick_b = act8 + [z_on, lane8 < 0]

        start = pl.multiple_of(p * obs, obs)
        rows = pl.ds(start, obs)
        wp = [[w_ref[t, pl.ds(pl.multiple_of(start + i * SUBS, SUBS), SUBS), :] for i in range(blocks)]
              for t in range(width)]
        shift = lax.rem(LANES - lax.rem(p, per) * obs, LANES)
        gram = w_ref[lax.div(p, per), rows, :]
        gram = pltpu.roll(gram, shift, 1)
        cols = [[jnp.broadcast_to(gram[i * SUBS:(i + 1) * SUBS, j:j + 1], (SUBS, LANES)) if i >= j // SUBS else None
                 for i in range(blocks)] for j in range(obs)]
        for k in range(obs):
            kb, ks = k // SUBS, k % SUBS
            col = cols[k]
            var = var_ref[b, k]
            pivot = spread(col[kb][ks:ks + 1, :])
            g = 1.0 / (pivot * inv + var)
            weight = g * inv
            beta = weight / (1.0 + jnp.sqrt(var * g))
            below = [None] * blocks
            below[kb] = jnp.where(sub8 > ks, col[kb], 0.0)
            for i in range(kb + 1, blocks):
                below[i] = col[i]
            for j in range(k + 1, obs):
                jb, js = j // SUBS, j % SUBS
                factor = weight * spread(col[jb][js:js + 1, :])
                for i in range(jb, blocks):
                    cols[j][i] = cols[j][i] - col[i] * factor
            for t in range(width):
                wk = spread(wp[t][kb][ks:ks + 1, :])
                both = jnp.where(pick_w[t], weight, beta) * wk
                single = jnp.where(pick_b[t], beta, 0.0) * wk
                right_ref[k:k + 1, t * LANES:(t + 1) * LANES] = both[:1]
                right_ref[obs + k:obs + k + 1, t * LANES:(t + 1) * LANES] = single[:1]
                for i in range(kb, blocks):
                    wp[t][i] = wp[t][i] - below[i] * both
        for t in range(tiles):
            for i in range(blocks):
                d = wp[t][i] * late[t]
                left_ref[i * SUBS:(i + 1) * SUBS, t * LANES:(t + 1) * LANES] = d * act[t]
                left_ref[obs + i * SUBS:obs + (i + 1) * SUBS, t * LANES:(t + 1) * LANES] = d * (1.0 - act[t])
        for i in range(blocks):
            at = pl.ds(pl.multiple_of(start + i * SUBS, SUBS), SUBS)
            z_ref[at, :] = wp[tiles][i] * mine_f
        gain = jnp.broadcast_to(right_ref[:obs, (width - 1) * LANES:(width - 1) * LANES + 1], (obs, LANES))
        v_ref[rows, :] = gain - right_ref[:obs, tiles * LANES:(tiles + 1) * LANES]

        @pl.when(p < batches - 1)
        def _():
            update = contract(left_ref[...], right_ref[...])
            for t in range(width):
                w_ref[t] = w_ref[t] - update[:, t * LANES:(t + 1) * LANES]

        return carry

    lax.fori_loop(0, batches, batch, 0)
    moved = contract(v_ref[...], z_ref[...])
    out_ref[...] = moved[members:members + half, :members]


def chain(own, oth, obs_value, obs_var, owner_tile, tile_mask, batch_order, tile):
    half, total = own.shape
    obs = obs_value.shape[1]
    width = total // LANES + 2
    f32 = jnp.float32
    return pl.pallas_call(
        chain_kernel,
        out_shape=jax.ShapeDtypeStruct((half, 2 * half), f32),
        in_specs=[SMEM] * 5 + [VMEM] * 3,
        out_specs=VMEM,
        scratch_shapes=[
            pltpu.VMEM((width, total, LANES), f32),
            pltpu.VMEM((2 * obs, total), f32),
            pltpu.VMEM((2 * obs, width * LANES), f32),
            pltpu.VMEM((total, LANES), f32),
            pltpu.VMEM((total, LANES), f32),
            pltpu.VMEM((obs_value.shape[0], LANES), f32),
        ],
        name="chain",
    )(batch_order, owner_tile, tile_mask, obs_var, tile, own, oth, obs_value)


def apply_kernel(mat_ref, own_ref, oth_ref, out_ref):
    half = mat_ref.shape[0]
    mat = mat_ref[...]
    high = mat.astype(jnp.bfloat16)
    low = (mat - high.astype(jnp.float32)).astype(jnp.bfloat16)
    left = jnp.concatenate(
        [jnp.concatenate([high, high], axis=1), jnp.concatenate([low, jnp.zeros_like(low)], axis=1)], axis=0)
    own = own_ref[0]
    x = jnp.concatenate([own, oth_ref[0]], axis=0)
    x_high = x.astype(jnp.bfloat16)
    x_low = (x - x_high.astype(jnp.float32)).astype(jnp.bfloat16)
    y = jnp.dot(left, jnp.concatenate([x_high, x_low], axis=0), preferred_element_type=jnp.float32)
    out_ref[0] = own + (y[:half] + y[half:])


def apply_matrix(mat, own, oth):
    chans, half, cells = own.shape
    spec = pl.BlockSpec((1, half, cells), lambda c: (c, 0, 0))
    return pl.pallas_call(
        apply_kernel,
        grid=(chans,),
        out_shape=jax.ShapeDtypeStruct(own.shape, jnp.float32),
        in_specs=[pl.BlockSpec(mat.shape, lambda c: (0, 0)), spec, spec],
        out_specs=spec,
        name="apply",
    )(mat, own, oth)


def body(ensemble, obs_site, obs_value, obs_var, owner_tile, tile_mask, batch_order):
    tile = lax.axis_index("tile").astype(jnp.int32).reshape(1)
    n_tile = lax.axis_size("tile")
    swap = [(0, 1), (1, 0)]
    ens = jnp.transpose(ensemble, (1, 0, 2))
    own = gather_rows(ens, obs_site, owner_tile, batch_order, tile)
    oth = lax.ppermute(own, "mem", swap)
    held, _ = lax.optimization_barrier((ens, own))
    bulk = lax.ppermute(held, "mem", swap)
    rows = jnp.concatenate([own, oth], axis=0)
    step = 1
    while step < n_tile:
        rows = rows + lax.ppermute(rows, "tile", [(i, i ^ step) for i in range(n_tile)])
        step *= 2
    half = own.shape[0]
    mat = chain(rows[:half], rows[half:], obs_value, obs_var, owner_tile, tile_mask, batch_order, tile)
    out = apply_matrix(mat, ens, bulk)
    return jnp.transpose(out, (1, 0, 2))


def solution(mesh):
    return jax.shard_map(
        body,
        mesh=mesh,
        in_specs=(P("mem", None, "tile"), P(), P(), P(), P(), P(), P()),
        out_specs=P("mem", None, "tile"),
        check_vma=False,
    )
```

time: 2170 us -> 85.8 us (0.04)
  loops' own time: 822 us -> 0 us
  blocking collectives: 501 us -> 0 us
  local copies, waits for them, and re-layouts: 355 us -> 0.62 us
  matrix products: 251 us -> 0 us
  other arithmetic: 184 us -> 1.56 us
  waiting for transfers between devices: 0.7 us -> 48.3 us
  between operations: 43.6 us -> 0.02 us
  Pallas kernels: 0 us -> 24.8 us
    another operation x8 -> x0, loops' own time: 822 us -> none  [batch_transform(): result, _ = lax.scan(assimilate, start_eye, (priors, values, variances))]
    psum x8 -> x0, blocking collectives: 465 us -> none  [from_root(): return lax.psum(block, axis)]
    dynamic_slice x514 -> x0, local copies, waits for them, and re-layouts: 317 us -> none  [the longest x512 316 us: batch_transform(): result, _ = lax.scan(assimilate, start_eye, (priors, values, variances))]
    dot_general x529 -> x0, matrix products: 251 us -> none  [the longest x256 207 us: assimilate(): y_row = jnp.dot(prior_row, transform, precision=highest)]
    reduce_sum x256 -> x0, other arithmetic: 161 us -> none  [assimilate(): sample_var = jnp.sum(spread * spread) / (count - 1)]
    ppermute x0 -> x6, waiting for transfers between devices: none -> 48.3 us  [the longest x1 40 us: body(): oth = lax.ppermute(own, 'mem', swap)]
    all_gather x8 -> x0, blocking collectives: 36.6 us -> none  [body(): obs_rows = lax.all_gather(local_rows, 'mem', axis=0, tiled=True)]
    gather x8 -> x0, local copies, waits for them, and re-layouts: 29.3 us -> none  [body(): local_rows = jnp.take(flat_state, obs_site[batch_id], axis=1)]
  transfers between devices with their start and end apart: 1 -> 6, of which waited for: 0 -> 5; matrix products, arithmetic and copies ran while one was open for 36% -> 3% of each run, Pallas kernels for 0% -> 18%
where the time goes in v1:
time: 85.8 us; the launch traced here: 85.4 us
  waiting for transfers between devices  48.3 us (56%)
  Pallas kernels  24.8 us (29%)
  starting transfers between devices  10.2 us (12%)
  other arithmetic  1.56 us (2%)
    ppermute x1, waiting for transfers between devices, body(): oth = lax.ppermute(own, 'mem', swap)  40 us
    pallas_call x1, Pallas kernels, chain(): pl.pallas_call(chain_kernel, out_shape=jax.ShapeDtypeStruct((half, 2 * ha...  15.4 us
    ppermute x4, waiting for transfers between devices, body(): lax.ppermute(rows, 'tile', [(i, i ^ step) for i in range(n_tile)])  8.22 us
    ppermute x4, starting transfers between devices, body(): lax.ppermute(rows, 'tile', [(i, i ^ step) for i in range(n_tile)])  7.14 us
    pallas_call x1, Pallas kernels, apply_matrix(): pl.pallas_call(apply_kernel, grid=(chans,), out_shape=jax.ShapeDtypeStruc...  6.29 us
    pallas_call x1, Pallas kernels, gather_rows(): pl.pallas_call(gather_kernel, out_shape=jax.ShapeDtypeStruct((ens.shape[1...  3.04 us
    ppermute x1, starting transfers between devices, body(): bulk = lax.ppermute(held, 'mem', swap)  3 us
  transfers between devices with their start and end apart: 6, of which 5 were waited for; matrix products, arithmetic and copies ran while one was open for 3% of the time, Pallas kernels for 18%

profile of v1, /device:TPU:0, one launch (start us, length us, event | category | flops | bytes accessed | tf_op | source)
XLA Modules:
  0.0 85.4 jit_solution(15019291535434445836)
XLA Ops:
  0.0 0.0 copy-start
  0.0 3.0 %gather_rows.1 = f32[32,256]{1,0:T(8,128)} custom-call(s32[8,32]{1,0:T(8,128)} %site_ref.1, s32[8]{0:T(128)} %owner_ref.3, s32[8]{0:T(128)} %order_ref.3, s32[1]{0:T(128)} %bitcast.tile_ref, f32[7,32,2048]{2,1,0:T(8,128)} %bitcast.3), custom_call_target="tpu_custom_call" | custom-call | tf_op jit(solution)/shard_map/gather_rows/pallas_call | solution.py:51
  3.0 0.0 copy-done
  3.0 3.0 %collective-permute-start.5 = (f32[7,32,2048]{2,1,0:T(8,128)S(1)}, f32[7,32,2048]{2,1,0:T(8,128)}, u32[]{:S(2)}, u32[]{:S(2)}) collective-permute-start(f32[7,32,2048]{2,1,0:T(8,128)S(1)} %bitcast.5), channel_id=1, source_target_pairs={{0,1},{1,0},{2,3},{3,2},{4,5},{5,4},{6,7},{7,6},{8,9},{9,8},{10,11... | collective-permute-start | bytes 5505032 | tf_op jit(solution)/shard_map/ppermute | solution.py:250
  6.0 0.0 collective-permute-start
  6.1 40.0 %collective-permute-done = f32[32,256]{1,0:T(8,128)S(1)} collective-permute-done((f32[32,256]{1,0:T(8,128)}, f32[32,256]{1,0:T(8,128)S(1)}, u32[]{:S(2)}, u32[]{:S(2)}) %collective-permute-start) | collective-permute-done | bytes 32800 | tf_op jit(solution)/shard_map/ppermute | solution.py:248
  46.1 0.8 pad_maximum_fusion
  46.9 0.0 collective-permute-start.1
  46.9 1.3 %collective-permute-done.1 = f32[64,256]{1,0:T(8,128)S(1)} collective-permute-done((f32[64,256]{1,0:T(8,128)S(1)}, f32[64,256]{1,0:T(8,128)S(1)}, u32[]{:S(2)}, u32[]{:S(2)}) %collective-permute-start.1) | collective-permute-done | bytes 65568 | tf_op jit(solution)/shard_map/ppermute | solution.py:254
  48.1 0.8 fusion
  48.9 2.1 %collective-permute-start.2 = (f32[64,256]{1,0:T(8,128)S(1)}, f32[64,256]{1,0:T(8,128)S(1)}, u32[]{:S(2)}, u32[]{:S(2)}) collective-permute-start(f32[64,256]{1,0:T(8,128)S(1)} %fusion), channel_id=1, source_target_pairs={{0,4},{2,6},{4,0},{6,2},{8,12},{10,14},{12,8},{14,10},{16,20},{18,... | collective-permute-start | bytes 196616 | tf_op jit(solution)/shard_map/ppermute | solution.py:254
  51.0 2.4 %collective-permute-done.2 = f32[64,256]{1,0:T(8,128)S(1)} collective-permute-done((f32[64,256]{1,0:T(8,128)S(1)}, f32[64,256]{1,0:T(8,128)S(1)}, u32[]{:S(2)}, u32[]{:S(2)}) %collective-permute-start.2) | collective-permute-done | bytes 65568 | tf_op jit(solution)/shard_map/ppermute | solution.py:254
  53.4 2.0 %collective-permute-start.3 = (f32[64,256]{1,0:T(8,128)S(1)}, f32[64,256]{1,0:T(8,128)S(1)}, u32[]{:S(2)}, u32[]{:S(2)}) collective-permute-start(f32[64,256]{1,0:T(8,128)S(1)} %add.13), channel_id=1, source_target_pairs={{0,8},{2,10},{4,12},{6,14},{8,0},{10,2},{12,4},{14,6},{16,24},{18,... | collective-permute-start | bytes 196616 | tf_op jit(solution)/shard_map/ppermute | solution.py:254
  55.5 2.3 %collective-permute-done.3 = f32[64,256]{1,0:T(8,128)S(1)} collective-permute-done((f32[64,256]{1,0:T(8,128)S(1)}, f32[64,256]{1,0:T(8,128)S(1)}, u32[]{:S(2)}, u32[]{:S(2)}) %collective-permute-start.3) | collective-permute-done | bytes 65568 | tf_op jit(solution)/shard_map/ppermute | solution.py:254
  57.8 3.0 %collective-permute-start.4 = (f32[64,256]{1,0:T(8,128)S(1)}, f32[64,256]{1,0:T(8,128)S(1)}, u32[]{:S(2)}, u32[]{:S(2)}) collective-permute-start(f32[64,256]{1,0:T(8,128)S(1)} %add.14), channel_id=1, source_target_pairs={{0,16},{2,18},{4,20},{6,22},{8,24},{10,26},{12,28},{14,30},{16,0},... | collective-permute-start | bytes 196616 | tf_op jit(solution)/shard_map/ppermute | solution.py:254
  60.8 2.2 %collective-permute-done.4 = f32[64,256]{1,0:T(8,128)S(1)} collective-permute-done((f32[64,256]{1,0:T(8,128)S(1)}, f32[64,256]{1,0:T(8,128)S(1)}, u32[]{:S(2)}, u32[]{:S(2)}) %collective-permute-start.4) | collective-permute-done | bytes 65568 | tf_op jit(solution)/shard_map/ppermute | solution.py:254
  63.1 0.6 fusion.1
  63.7 15.4 %chain.1.mat_ref = f32[32,64]{1,0:T(8,128)} custom-call(s32[8]{0:T(128)} %order_ref.3, s32[8]{0:T(128)} %owner_ref.3, s32[8,16]{1,0:T(8,128)} %mask_ref.1, f32[8,32]{1,0:T(8,128)} %var_ref.1, s32[1]{0:T(128)} %bitcast.tile_ref, f32[32,256]{1,0:T(8,128)} %get-tuple-element.8.own_ref, f32[32,256]{1,0:T(8,128)} %get-tuple-element.7.oth_ref, f32[8,32]{1,0:T(8,128)} %val_ref.1), custom_call_target="tpu_custom_call" | custom-call | tf_op jit(solution)/shard_map/chain/pallas_call | solution.py:197
  79.1 0.0 collective-permute-done.5.oth_ref
  79.1 6.3 %apply.1 = f32[7,32,2048]{2,1,0:T(8,128)} custom-call(f32[32,64]{1,0:T(8,128)} %chain.1.mat_ref, f32[7,32,2048]{2,1,0:T(8,128)} %bitcast.4, f32[7,32,2048]{2,1,0:T(8,128)} %collective-permute-done.5.oth_ref), custom_call_target="tpu_custom_call" | custom-call | tf_op jit(solution)/shard_map/apply/pallas_call | solution.py:232
  (3 shorter events, 0.0 us)
Async XLA Ops:
  0.0 3.0 %copy-start = (f32[32,7,2048]{2,0,1:T(8,128)S(1)}, f32[32,7,2048]{2,0,1:T(8,128)}, u32[]{:S(2)}) copy-start(f32[32,7,2048]{2,0,1:T(8,128)} %param.7) | copy-start | bytes 5505028
  3.0 76.1 %collective-permute-start.5 = (f32[7,32,2048]{2,1,0:T(8,128)S(1)}, f32[7,32,2048]{2,1,0:T(8,128)}, u32[]{:S(2)}, u32[]{:S(2)}) collective-permute-start(f32[7,32,2048]{2,1,0:T(8,128)S(1)} %bitcast.5), channel_id=1, source_target_pairs={{0,1},{1,0},{2,3},{3,2},{4,5},{5,4},{6,7},{7,6},{8,9},{9,8},{10,11... | collective-permute-start | bytes 5505032 | tf_op jit(solution)/shard_map/ppermute | solution.py:250
  6.0 40.1 %collective-permute-start = (f32[32,256]{1,0:T(8,128)}, f32[32,256]{1,0:T(8,128)S(1)}, u32[]{:S(2)}, u32[]{:S(2)}) collective-permute-start(f32[32,256]{1,0:T(8,128)} %gather_rows.1), channel_id=1, source_target_pairs={{0,1},{1,0},{2,3},{3,2},{4,5},{5,4},{6,7},{7,6},{8,9},{9,8},{10,11... | collective-permute-start | bytes 98312 | tf_op jit(solution)/shard_map/ppermute | solution.py:248
  46.9 1.3 %collective-permute-start.1 = (f32[64,256]{1,0:T(8,128)S(1)}, f32[64,256]{1,0:T(8,128)S(1)}, u32[]{:S(2)}, u32[]{:S(2)}) collective-permute-start(f32[64,256]{1,0:T(8,128)S(1)} %pad_maximum_fusion), channel_id=1, source_target_pairs={{0,2},{2,0},{4,6},{6,4},{8,10},{10,8},{12,14},{14,12},{16,18},{18,... | collective-permute-start | bytes 196616 | tf_op jit(solution)/shard_map/ppermute | solution.py:254
  48.9 4.5 %collective-permute-start.2 = (f32[64,256]{1,0:T(8,128)S(1)}, f32[64,256]{1,0:T(8,128)S(1)}, u32[]{:S(2)}, u32[]{:S(2)}) collective-permute-start(f32[64,256]{1,0:T(8,128)S(1)} %fusion), channel_id=1, source_target_pairs={{0,4},{2,6},{4,0},{6,2},{8,12},{10,14},{12,8},{14,10},{16,20},{18,... | collective-permute-start | bytes 196616 | tf_op jit(solution)/shard_map/ppermute | solution.py:254
  53.4 4.3 %collective-permute-start.3 = (f32[64,256]{1,0:T(8,128)S(1)}, f32[64,256]{1,0:T(8,128)S(1)}, u32[]{:S(2)}, u32[]{:S(2)}) collective-permute-start(f32[64,256]{1,0:T(8,128)S(1)} %add.13), channel_id=1, source_target_pairs={{0,8},{2,10},{4,12},{6,14},{8,0},{10,2},{12,4},{14,6},{16,24},{18,... | collective-permute-start | bytes 196616 | tf_op jit(solution)/shard_map/ppermute | solution.py:254
  57.8 5.3 %collective-permute-start.4 = (f32[64,256]{1,0:T(8,128)S(1)}, f32[64,256]{1,0:T(8,128)S(1)}, u32[]{:S(2)}, u32[]{:S(2)}) collective-permute-start(f32[64,256]{1,0:T(8,128)S(1)} %add.14), channel_id=1, source_target_pairs={{0,16},{2,18},{4,20},{6,22},{8,24},{10,26},{12,28},{14,30},{16,0},... | collective-permute-start | bytes 196616 | tf_op jit(solution)/shard_map/ppermute | solution.py:254

commit v2 on v1

--- a/solution.py
+++ b/solution.py
@@ -6,6 +6,7 @@
 from jax.experimental import pallas as pl
 from jax.experimental.pallas import tpu as pltpu
 from jax.sharding import PartitionSpec as P
+
 
 LANES = 128
 SUBS = 8
@@ -53,6 +54,7 @@
         out_shape=jax.ShapeDtypeStruct((ens.shape[1], batches * obs), jnp.float32),
         in_specs=[SMEM, SMEM, SMEM, SMEM, VMEM],
         out_specs=VMEM,
+        compiler_params=pltpu.CompilerParams(vmem_limit_bytes=4 << 20),
         name="gather_rows",
     )(obs_site, owner_tile, batch_order, tile, ens)
 
@@ -61,11 +63,11 @@
     return jnp.broadcast_to(row, (SUBS, row.shape[1]))
 
 
-def chain_kernel(order_ref, owner_ref, mask_ref, var_ref, tile_ref, own_ref, oth_ref, val_ref,
+def chain_kernel(order_ref, owner_ref, mask_ref, var_ref, tile_ref, raw_ref, val_ref,
                  out_ref, w_ref, left_ref, right_ref, z_ref, v_ref, val_s):
     batches, obs = val_ref.shape
-    half = own_ref.shape[0]
-    members = 2 * half
+    members = raw_ref.shape[0]
+    half = members // 2
     total = batches * obs
     tiles = total // LANES
     per = LANES // obs
@@ -92,7 +94,7 @@
         values.append(row)
     values = jnp.concatenate(values, axis=1)
 
-    raw = jnp.concatenate([own_ref[...], oth_ref[...]], axis=0)
+    raw = raw_ref[...]
     mean = jnp.sum(raw, axis=0, keepdims=True) * (1.0 / members)
     anom = raw - mean
     first = lax.broadcasted_iota(jnp.int32, (SUBS, total), 0) == 0
@@ -189,15 +191,16 @@
     out_ref[...] = moved[members:members + half, :members]
 
 
-def chain(own, oth, obs_value, obs_var, owner_tile, tile_mask, batch_order, tile):
-    half, total = own.shape
+def chain(rows, obs_value, obs_var, owner_tile, tile_mask, batch_order, tile):
+    members, total = rows.shape
+    half = members // 2
     obs = obs_value.shape[1]
     width = total // LANES + 2
     f32 = jnp.float32
     return pl.pallas_call(
         chain_kernel,
-        out_shape=jax.ShapeDtypeStruct((half, 2 * half), f32),
-        in_specs=[SMEM] * 5 + [VMEM] * 3,
+        out_shape=jax.ShapeDtypeStruct((half, members), f32),
+        in_specs=[SMEM] * 5 + [VMEM] * 2,
         out_specs=VMEM,
         scratch_shapes=[
             pltpu.VMEM((width, total, LANES), f32),
@@ -207,36 +210,58 @@
             pltpu.VMEM((total, LANES), f32),
             pltpu.VMEM((obs_value.shape[0], LANES), f32),
         ],
+        compiler_params=pltpu.CompilerParams(vmem_limit_bytes=8 << 20),
         name="chain",
-    )(batch_order, owner_tile, tile_mask, obs_var, tile, own, oth, obs_value)
-
-
-def apply_kernel(mat_ref, own_ref, oth_ref, out_ref):
+    )(batch_order, owner_tile, tile_mask, obs_var, tile, rows, obs_value)
+
+
+def apply_kernel(mat_ref, own_ref, *rest):
+    oth_refs, out_ref = rest[:-1], rest[-1]
     half = mat_ref.shape[0]
+    oth = oth_refs[0][0]
     mat = mat_ref[...]
     high = mat.astype(jnp.bfloat16)
     low = (mat - high.astype(jnp.float32)).astype(jnp.bfloat16)
     left = jnp.concatenate(
         [jnp.concatenate([high, high], axis=1), jnp.concatenate([low, jnp.zeros_like(low)], axis=1)], axis=0)
     own = own_ref[0]
-    x = jnp.concatenate([own, oth_ref[0]], axis=0)
+    x = jnp.concatenate([own, oth], axis=0)
     x_high = x.astype(jnp.bfloat16)
     x_low = (x - x_high.astype(jnp.float32)).astype(jnp.bfloat16)
     y = jnp.dot(left, jnp.concatenate([x_high, x_low], axis=0), preferred_element_type=jnp.float32)
     out_ref[0] = own + (y[:half] + y[half:])
 
 
-def apply_matrix(mat, own, oth):
-    chans, half, cells = own.shape
+def apply_first(mat_ref, own_ref, oth_ref, out_ref):
+    apply_kernel(mat_ref, own_ref, oth_ref, out_ref)
+
+
+def apply_next(mat_ref, own_ref, oth_ref, prev_ref, out_ref):
+    apply_kernel(mat_ref, own_ref, oth_ref, out_ref)
+
+
+def apply_matrix(mat, own, oth, start, out):
+    _, half, cells = own.shape
+    here = oth.shape[0]
     spec = pl.BlockSpec((1, half, cells), lambda c: (c, 0, 0))
+    shifted = pl.BlockSpec((1, half, cells), lambda c: (c + start, 0, 0))
+    args = [mat, own, oth]
+    in_specs = [pl.BlockSpec(mat.shape, lambda c: (0, 0)), shifted, spec]
+    alias = {}
+    if out is not None:
+        args.append(out)
+        in_specs.append(pl.BlockSpec(memory_space=pl.ANY))
+        alias = {3: 0}
     return pl.pallas_call(
-        apply_kernel,
-        grid=(chans,),
+        apply_first if out is None else apply_next,
+        grid=(here,),
         out_shape=jax.ShapeDtypeStruct(own.shape, jnp.float32),
-        in_specs=[pl.BlockSpec(mat.shape, lambda c: (0, 0)), spec, spec],
-        out_specs=spec,
+        in_specs=in_specs,
+        out_specs=shifted,
+        input_output_aliases=alias,
+        compiler_params=pltpu.CompilerParams(vmem_limit_bytes=8 << 20),
         name="apply",
-    )(mat, own, oth)
+    )(*args)
 
 
 def body(ensemble, obs_site, obs_value, obs_var, owner_tile, tile_mask, batch_order):
@@ -244,18 +269,21 @@
     n_tile = lax.axis_size("tile")
     swap = [(0, 1), (1, 0)]
     ens = jnp.transpose(ensemble, (1, 0, 2))
+    chans = ens.shape[0]
+    first = lax.ppermute(ens[:1], "mem", swap)
     own = gather_rows(ens, obs_site, owner_tile, batch_order, tile)
     oth = lax.ppermute(own, "mem", swap)
-    held, _ = lax.optimization_barrier((ens, own))
-    bulk = lax.ppermute(held, "mem", swap)
+    mid = lax.ppermute(ens[1:chans - 1], "mem", swap)
+    last = lax.ppermute(ens[chans - 1:], "mem", swap)
     rows = jnp.concatenate([own, oth], axis=0)
     step = 1
     while step < n_tile:
         rows = rows + lax.ppermute(rows, "tile", [(i, i ^ step) for i in range(n_tile)])
         step *= 2
-    half = own.shape[0]
-    mat = chain(rows[:half], rows[half:], obs_value, obs_var, owner_tile, tile_mask, batch_order, tile)
-    out = apply_matrix(mat, ens, bulk)
+    mat = chain(rows, obs_value, obs_var, owner_tile, tile_mask, batch_order, tile)
+    out = apply_matrix(mat, ens, first, 0, None)
+    out = apply_matrix(mat, ens, mid, 1, out)
+    out = apply_matrix(mat, ens, last, chans - 1, out)
     return jnp.transpose(out, (1, 0, 2))
 
 

time: 85.8 us -> 71.1 us (0.83)
  waiting for transfers between devices: 48.3 us -> 35.8 us
  Pallas kernels: 24.8 us -> 20.5 us
  local copies, waits for them, and re-layouts: 0.62 us -> 2.71 us
  other arithmetic: 1.56 us -> 0.04 us
  starting transfers between devices: 10.2 us -> 11.7 us
    ppermute x1, waiting for transfers between devices: 40 us -> 28.5 us  [body(): oth = lax.ppermute(own, 'mem', swap)]
    pallas_call x2 -> x4, Pallas kernels: 21.7 us -> 19.5 us  [the longest x1 14.6 us: chain(): pl.pallas_call(chain_kernel, out_shape=jax.ShapeDtypeStruct((half, member...]
    ppermute x1 -> x3, starting transfers between devices: 3 us -> 5.1 us  [the longest x1 3.01 us: body(): mid = lax.ppermute(ens[1:chans - 1], 'mem', swap)]
    slice x1 -> x2, local copies, waits for them, and re-layouts: 0.62 us -> 2.68 us  [the longest x1 2.64 us: body(): mid = lax.ppermute(ens[1:chans - 1], 'mem', swap)]
    pallas_call x1, Pallas kernels: 3.04 us -> 1.08 us  [gather_rows(): pl.pallas_call(gather_kernel, out_shape=jax.ShapeDtypeStruct((ens.shape[1...]
  transfers between devices with their start and end apart: 6 -> 8, of which waited for: 5 -> 4; matrix products, arithmetic and copies ran while one was open for 3% -> 0% of each run, Pallas kernels for 18% -> 28%
where the time goes in v2:
time: 71.1 us; the launch traced here: 71 us
  waiting for transfers between devices  35.8 us (50%)
  Pallas kernels  20.5 us (29%)
  starting transfers between devices  11.7 us (16%)
  local copies, waits for them, and re-layouts  2.71 us (4%)
    ppermute x1, waiting for transfers between devices, body(): oth = lax.ppermute(own, 'mem', swap)  28.5 us
    pallas_call x1, Pallas kernels, chain(): pl.pallas_call(chain_kernel, out_shape=jax.ShapeDtypeStruct((half, member...  14.6 us
    ppermute x4, waiting for transfers between devices, body(): lax.ppermute(rows, 'tile', [(i, i ^ step) for i in range(n_tile)])  7.37 us
    ppermute x4, starting transfers between devices, body(): lax.ppermute(rows, 'tile', [(i, i ^ step) for i in range(n_tile)])  6.53 us
    pallas_call x3, Pallas kernels, apply_matrix(): pl.pallas_call(apply_first if out is None else apply_next, grid=(here,),...  4.88 us
    ppermute x1, starting transfers between devices, body(): mid = lax.ppermute(ens[1:chans - 1], 'mem', swap)  3.01 us
    slice x1, local copies, waits for them, and re-layouts, body(): mid = lax.ppermute(ens[1:chans - 1], 'mem', swap)  2.64 us
    ppermute x1, starting transfers between devices, body(): first = lax.ppermute(ens[:1], 'mem', swap)  1.81 us
  transfers between devices with their start and end apart: 8, of which 4 were waited for; matrix products, arithmetic and copies ran while one was open for 0% of the time, Pallas kernels for 28%

profile of v2, /device:TPU:0, one launch (start us, length us, event | category | flops | bytes accessed | tf_op | source)
XLA Modules:
  0.0 71.0 jit_solution(3108308896557026842)
XLA Ops:
  0.0 0.0 copy-start
  0.0 0.0 copy-start.5
  0.0 0.0 copy-start.6
  0.0 0.0 copy-start.1
  0.0 2.6 %slice.13 = f32[5,32,2048]{2,1,0:T(8,128)} slice(f32[7,32,2048]{2,1,0:T(8,128)} %bitcast.3), slice={[1:6], [0:32], [0:2048]} | slice | bytes 2621440 | tf_op jit(solution)/shard_map/slice | solution.py:276
  2.7 3.0 %collective-permute-start.6 = (f32[5,32,2048]{2,1,0:T(8,128)}, f32[5,32,2048]{2,1,0:T(8,128)S(1)}, u32[]{:S(2)}, u32[]{:S(2)}) collective-permute-start(f32[5,32,2048]{2,1,0:T(8,128)} %slice.13), channel_id=1, source_target_pairs={{0,1},{1,0},{2,3},{3,2},{4,5},{5,4},{6,7},{7,6},{8,9},{9,8},{10,11... | collective-permute-start | bytes 3932168 | tf_op jit(solution)/shard_map/ppermute | solution.py:276
  5.7 0.0 copy-done
  5.7 0.0 copy-done.5
  5.7 0.0 copy-done.6
  5.7 0.0 copy-done.1
  5.7 0.0 copy-start.2
  5.7 0.0 copy-start.3
  5.7 0.0 copy-start.4
  5.7 1.1 %gather_rows.1 = f32[32,256]{1,0:T(8,128)S(1)} custom-call(s32[8,32]{1,0:T(8,128)S(1)} %copy-done.1, s32[8]{0:T(128)S(1)} %copy-done.6, s32[8]{0:T(128)S(1)} %copy-done.5, s32[1]{0:T(128)} %bitcast.tile_ref, f32[7,32,2048]{2,1,0:T(8,128)S(1)} %bitcast.4), custom_call_target="tpu_custom_call" | custom-call | tf_op jit(solution)/shard_map/gather_rows/pallas_call | solution.py:52
  6.8 0.1 collective-permute-start
  6.9 28.5 %collective-permute-done = f32[32,256]{1,0:T(8,128)S(1)} collective-permute-done((f32[32,256]{1,0:T(8,128)S(1)}, f32[32,256]{1,0:T(8,128)S(1)}, u32[]{:S(2)}, u32[]{:S(2)}) %collective-permute-start) | collective-permute-done | bytes 32800 | tf_op jit(solution)/shard_map/ppermute | solution.py:275
  35.4 0.0 collective-permute-start.1
  35.4 1.8 %collective-permute-start.7 = (f32[1,32,2048]{2,1,0:T(8,128)S(1)}, f32[1,32,2048]{2,1,0:T(8,128)S(1)}, u32[]{:S(2)}, u32[]{:S(2)}) collective-permute-start(f32[1,32,2048]{2,1,0:T(8,128)S(1)} %get-tuple-element.5), channel_id=1, source_target_pairs={{0,1},{1,0},{2,3},{3,2},{4,5},{5,4},{6,7},{7,6},{8,9},{9,8},{10,11... | collective-permute-start | bytes 786440 | tf_op jit(solution)/shard_map/ppermute | solution.py:273
  37.2 0.3 collective-permute-start.5
  37.5 0.0 collective-permute-done.1
  37.5 1.8 %collective-permute-start.2 = (f32[64,256]{1,0:T(8,128)S(1)}, f32[64,256]{1,0:T(8,128)S(1)}, u32[]{:S(2)}, u32[]{:S(2)}) collective-permute-start(f32[64,256]{1,0:T(8,128)S(1)} %fusion), channel_id=1, source_target_pairs={{0,4},{2,6},{4,0},{6,2},{8,12},{10,14},{12,8},{14,10},{16,20},{18,... | collective-permute-start | bytes 196616 | tf_op jit(solution)/shard_map/ppermute | solution.py:281
  39.3 2.6 %collective-permute-done.2 = f32[64,256]{1,0:T(8,128)S(1)} collective-permute-done((f32[64,256]{1,0:T(8,128)S(1)}, f32[64,256]{1,0:T(8,128)S(1)}, u32[]{:S(2)}, u32[]{:S(2)}) %collective-permute-start.2) | collective-permute-done | bytes 65568 | tf_op jit(solution)/shard_map/ppermute | solution.py:281
  41.9 1.9 %collective-permute-start.3 = (f32[64,256]{1,0:T(8,128)S(1)}, f32[64,256]{1,0:T(8,128)S(1)}, u32[]{:S(2)}, u32[]{:S(2)}) collective-permute-start(f32[64,256]{1,0:T(8,128)S(1)} %add.13), channel_id=1, source_target_pairs={{0,8},{2,10},{4,12},{6,14},{8,0},{10,2},{12,4},{14,6},{16,24},{18,... | collective-permute-start | bytes 196616 | tf_op jit(solution)/shard_map/ppermute | solution.py:281
  43.7 2.5 %collective-permute-done.3 = f32[64,256]{1,0:T(8,128)S(1)} collective-permute-done((f32[64,256]{1,0:T(8,128)S(1)}, f32[64,256]{1,0:T(8,128)S(1)}, u32[]{:S(2)}, u32[]{:S(2)}) %collective-permute-start.3) | collective-permute-done | bytes 65568 | tf_op jit(solution)/shard_map/ppermute | solution.py:281
  46.2 2.9 %collective-permute-start.4 = (f32[64,256]{1,0:T(8,128)S(1)}, f32[64,256]{1,0:T(8,128)S(1)}, u32[]{:S(2)}, u32[]{:S(2)}) collective-permute-start(f32[64,256]{1,0:T(8,128)S(1)} %add.14), channel_id=1, source_target_pairs={{0,16},{2,18},{4,20},{6,22},{8,24},{10,26},{12,28},{14,30},{16,0},... | collective-permute-start | bytes 196616 | tf_op jit(solution)/shard_map/ppermute | solution.py:281
  49.1 2.4 %collective-permute-done.4 = f32[64,256]{1,0:T(8,128)S(1)} collective-permute-done((f32[64,256]{1,0:T(8,128)S(1)}, f32[64,256]{1,0:T(8,128)S(1)}, u32[]{:S(2)}, u32[]{:S(2)}) %collective-permute-start.4) | collective-permute-done | bytes 65568 | tf_op jit(solution)/shard_map/ppermute | solution.py:281
  51.4 0.0 copy-done.2
  51.5 0.0 copy-done.3
  51.5 0.0 copy-done.4
  51.5 14.6 %chain.1.mat_ref = f32[32,64]{1,0:T(8,128)S(1)} custom-call(s32[8]{0:T(128)S(1)} %copy-done.5, s32[8]{0:T(128)S(1)} %copy-done.6, s32[8,16]{1,0:T(8,128)S(1)} %copy-done.2, f32[8,32]{1,0:T(8,128)S(1)} %copy-done.3, s32[1]{0:T(128)} %bitcast.tile_ref, f32[64,256]{1,0:T(8,128)S(1)} %add.15.raw_ref, f32[8,32]{1,0:T(8,128)S(1)} %copy-done.4), custom_call_target="tpu_custom_call" | custom-call | tf_op jit(solution)/shard_map/chain/pallas_call | solution.py:200
  66.1 0.0 collective-permute-done.7.oth_ref
  66.1 1.0 %apply.3.prev_ref = f32[7,32,2048]{2,1,0:T(8,128)} custom-call(f32[32,64]{1,0:T(8,128)S(1)} %chain.1.mat_ref, f32[7,32,2048]{2,1,0:T(8,128)S(1)} %bitcast.6, f32[1,32,2048]{2,1,0:T(8,128)S(1)} %collective-permute-done.7.oth_ref), custom_call_target="tpu_custom_call" | custom-call | tf_op jit(solution)/shard_map/apply/pallas_call | solution.py:255
  67.1 0.0 collective-permute-done.6.oth_ref
  67.1 2.9 %apply.4.prev_ref = f32[7,32,2048]{2,1,0:T(8,128)} custom-call(f32[32,64]{1,0:T(8,128)S(1)} %chain.1.mat_ref, f32[7,32,2048]{2,1,0:T(8,128)S(1)} %bitcast.7, f32[5,32,2048]{2,1,0:T(8,128)S(1)} %collective-permute-done.6.oth_ref, f32[7,32,2048]{2,1,0:T(8,128)} %apply.3.prev_ref), custom_call_target="tpu_custom_call", output_to_operand_aliasing={{}: (3, {})} | custom-call | tf_op jit(solution)/shard_map/apply/pallas_call | solution.py:255
  70.0 0.0 collective-permute-done.5.oth_ref
  70.0 1.0 %apply.5 = f32[7,32,2048]{2,1,0:T(8,128)} custom-call(f32[32,64]{1,0:T(8,128)S(1)} %chain.1.mat_ref, f32[7,32,2048]{2,1,0:T(8,128)S(1)} %bitcast.8, f32[1,32,2048]{2,1,0:T(8,128)S(1)} %collective-permute-done.5.oth_ref, f32[7,32,2048]{2,1,0:T(8,128)} %apply.4.prev_ref), custom_call_target="tpu_custom_call", output_to_operand_aliasing={{}: (3, {})} | custom-call | tf_op jit(solution)/shard_map/apply/pallas_call | solution.py:255
  (6 shorter events, 0.1 us)
Async XLA Ops:
  0.0 5.7 %copy-start = (f32[32,7,2048]{2,0,1:T(8,128)S(1)}, f32[32,7,2048]{2,0,1:T(8,128)}, u32[]{:S(2)}) copy-start(f32[32,7,2048]{2,0,1:T(8,128)} %param.7) | copy-start | bytes 5505028
  0.0 5.7 %copy-start.5 = (s32[8]{0:T(128)S(1)}, s32[8]{0:T(128)}, u32[]{:S(2)}) copy-start(s32[8]{0:T(128)} %order_ref.3) | copy-start | bytes 100
  0.0 5.7 %copy-start.6 = (s32[8]{0:T(128)S(1)}, s32[8]{0:T(128)}, u32[]{:S(2)}) copy-start(s32[8]{0:T(128)} %owner_ref.3) | copy-start | bytes 100
  0.0 5.7 %copy-start.1 = (s32[8,32]{1,0:T(8,128)S(1)}, s32[8,32]{1,0:T(8,128)}, u32[]{:S(2)}) copy-start(s32[8,32]{1,0:T(8,128)} %site_ref.1) | copy-start | bytes 3076
  2.7 64.4 %collective-permute-start.6 = (f32[5,32,2048]{2,1,0:T(8,128)}, f32[5,32,2048]{2,1,0:T(8,128)S(1)}, u32[]{:S(2)}, u32[]{:S(2)}) collective-permute-start(f32[5,32,2048]{2,1,0:T(8,128)} %slice.13), channel_id=1, source_target_pairs={{0,1},{1,0},{2,3},{3,2},{4,5},{5,4},{6,7},{7,6},{8,9},{9,8},{10,11... | collective-permute-start | bytes 3932168 | tf_op jit(solution)/shard_map/ppermute | solution.py:276
  5.7 45.8 %copy-start.2 = (s32[8,16]{1,0:T(8,128)S(1)}, s32[8,16]{1,0:T(8,128)}, u32[]{:S(2)}) copy-start(s32[8,16]{1,0:T(8,128)} %mask_ref.1) | copy-start | bytes 1540
  5.7 45.8 %copy-start.3 = (f32[8,32]{1,0:T(8,128)S(1)}, f32[8,32]{1,0:T(8,128)}, u32[]{:S(2)}) copy-start(f32[8,32]{1,0:T(8,128)} %var_ref.1) | copy-start | bytes 3076
  5.7 45.8 %copy-start.4 = (f32[8,32]{1,0:T(8,128)S(1)}, f32[8,32]{1,0:T(8,128)}, u32[]{:S(2)}) copy-start(f32[8,32]{1,0:T(8,128)} %val_ref.1) | copy-start | bytes 3076
  6.8 28.6 %collective-permute-start = (f32[32,256]{1,0:T(8,128)S(1)}, f32[32,256]{1,0:T(8,128)S(1)}, u32[]{:S(2)}, u32[]{:S(2)}) collective-permute-start(f32[32,256]{1,0:T(8,128)S(1)} %gather_rows.1), channel_id=1, source_target_pairs={{0,1},{1,0},{2,3},{3,2},{4,5},{5,4},{6,7},{7,6},{8,9},{9,8},{10,11... | collective-permute-start | bytes 98312 | tf_op jit(solution)/shard_map/ppermute | solution.py:275
  35.4 2.1 %collective-permute-start.1 = (f32[64,256]{1,0:T(8,128)S(1)}, f32[64,256]{1,0:T(8,128)S(1)}, u32[]{:S(2)}, u32[]{:S(2)}) collective-permute-start(f32[64,256]{1,0:T(8,128)S(1)} %pad_maximum_fusion), channel_id=1, source_target_pairs={{0,2},{2,0},{4,6},{6,4},{8,10},{10,8},{12,14},{14,12},{16,18},{18,... | collective-permute-start | bytes 196616 | tf_op jit(solution)/shard_map/ppermute | solution.py:281
  35.4 30.7 %collective-permute-start.7 = (f32[1,32,2048]{2,1,0:T(8,128)S(1)}, f32[1,32,2048]{2,1,0:T(8,128)S(1)}, u32[]{:S(2)}, u32[]{:S(2)}) collective-permute-start(f32[1,32,2048]{2,1,0:T(8,128)S(1)} %get-tuple-element.5), channel_id=1, source_target_pairs={{0,1},{1,0},{2,3},{3,2},{4,5},{5,4},{6,7},{7,6},{8,9},{9,8},{10,11... | collective-permute-start | bytes 786440 | tf_op jit(solution)/shard_map/ppermute | solution.py:273
  37.2 32.8 %collective-permute-start.5 = (f32[1,32,2048]{2,1,0:T(8,128)S(1)}, f32[1,32,2048]{2,1,0:T(8,128)S(1)}, u32[]{:S(2)}, u32[]{:S(2)}) collective-permute-start(f32[1,32,2048]{2,1,0:T(8,128)S(1)} %get-tuple-element.6), channel_id=1, source_target_pairs={{0,1},{1,0},{2,3},{3,2},{4,5},{5,4},{6,7},{7,6},{8,9},{9,8},{10,11... | collective-permute-start | bytes 786440 | tf_op jit(solution)/shard_map/ppermute | solution.py:277
  37.5 4.3 %collective-permute-start.2 = (f32[64,256]{1,0:T(8,128)S(1)}, f32[64,256]{1,0:T(8,128)S(1)}, u32[]{:S(2)}, u32[]{:S(2)}) collective-permute-start(f32[64,256]{1,0:T(8,128)S(1)} %fusion), channel_id=1, source_target_pairs={{0,4},{2,6},{4,0},{6,2},{8,12},{10,14},{12,8},{14,10},{16,20},{18,... | collective-permute-start | bytes 196616 | tf_op jit(solution)/shard_map/ppermute | solution.py:281
  41.9 4.3 %collective-permute-start.3 = (f32[64,256]{1,0:T(8,128)S(1)}, f32[64,256]{1,0:T(8,128)S(1)}, u32[]{:S(2)}, u32[]{:S(2)}) collective-permute-start(f32[64,256]{1,0:T(8,128)S(1)} %add.13), channel_id=1, source_target_pairs={{0,8},{2,10},{4,12},{6,14},{8,0},{10,2},{12,4},{14,6},{16,24},{18,... | collective-permute-start | bytes 196616 | tf_op jit(solution)/shard_map/ppermute | solution.py:281
  46.2 5.2 %collective-permute-start.4 = (f32[64,256]{1,0:T(8,128)S(1)}, f32[64,256]{1,0:T(8,128)S(1)}, u32[]{:S(2)}, u32[]{:S(2)}) collective-permute-start(f32[64,256]{1,0:T(8,128)S(1)} %add.14), channel_id=1, source_target_pairs={{0,16},{2,18},{4,20},{6,22},{8,24},{10,26},{12,28},{14,30},{16,0},... | collective-permute-start | bytes 196616 | tf_op jit(solution)/shard_map/ppermute | solution.py:281

commit v3 on v1

--- a/solution.py
+++ b/solution.py
@@ -7,65 +7,128 @@
 from jax.experimental.pallas import tpu as pltpu
 from jax.sharding import PartitionSpec as P
 
+
 LANES = 128
 SUBS = 8
 SMEM = pl.BlockSpec(memory_space=pltpu.SMEM)
 VMEM = pl.BlockSpec(memory_space=pltpu.VMEM)
-
-
-def gather_kernel(site_ref, owner_ref, order_ref, tile_ref, ens_ref, out_ref):
-    batches, obs = site_ref.shape
-    cells = ens_ref.shape[2]
-    members = ens_ref.shape[1]
+ANY = pl.BlockSpec(memory_space=pl.ANY)
+
+
+def hbm(x):
+    return pltpu.with_memory_space_constraint(x, pltpu.HBM)
+
+
+def vmem(x):
+    return pltpu.with_memory_space_constraint(x, pltpu.VMEM)
+
+
+def first_kernel(units_hbm, first_ref, sem):
+    copy = pltpu.make_async_copy(units_hbm.at[pl.ds(0, first_ref.shape[0])], first_ref, sem)
+    copy.start()
+    copy.wait()
+
+
+def first_units(units, count):
+    return pl.pallas_call(
+        first_kernel,
+        out_shape=pltpu.VMEM((count,) + units.shape[1:], jnp.float32),
+        in_specs=[ANY],
+        out_specs=VMEM,
+        scratch_shapes=[pltpu.SemaphoreType.DMA],
+        name="first_units",
+    )(hbm(units))
+
+
+def gather_kernel(site_hbm, owner_hbm, order_hbm, units_hbm, rows_ref, main_hbm, last_ref,
+                  held_ref, site_ref, owner_ref, order_ref, sem):
+    batches, obs = site_hbm.shape
+    count, half, cells = units_hbm.shape
     per = LANES // obs
-    lane = lax.broadcasted_iota(jnp.int32, (members, LANES), 1)
-    out_ref[...] = jnp.zeros_like(out_ref)
+    tail = last_ref.shape[0]
+    middle = main_hbm.shape[0]
+    state = pltpu.make_async_copy(units_hbm, held_ref, sem.at[0])
+    small = [
+        pltpu.make_async_copy(site_hbm, site_ref, sem.at[1]),
+        pltpu.make_async_copy(owner_hbm, owner_ref, sem.at[2]),
+        pltpu.make_async_copy(order_hbm, order_ref, sem.at[3]),
+    ]
+    end = pltpu.make_async_copy(units_hbm.at[pl.ds(count - tail, tail)], last_ref, sem.at[4])
+    for copy in small + [state, end]:
+        copy.start()
+    tile = lax.axis_index("tile")
+    lane = lax.broadcasted_iota(jnp.int32, (half, LANES), 1)
+    rows_ref[...] = jnp.zeros_like(rows_ref)
+    state.wait()
+    out = pltpu.make_async_copy(held_ref.at[pl.ds(count - tail - middle, middle)], main_hbm, sem.at[5])
+    out.start()
+    for copy in small:
+        copy.wait()
 
     def one(p, carry):
         b = order_ref[p]
 
-        @pl.when(owner_ref[b] == tile_ref[0])
+        @pl.when(owner_ref[b] == tile)
         def _():
             base = lax.rem(p, per) * obs
             spot = pl.ds(pl.multiple_of(lax.div(p, per) * LANES, LANES), LANES)
-            acc = out_ref[:, spot]
+            acc = [rows_ref[h * half:(h + 1) * half, spot] for h in range(2)]
             for k in range(obs):
                 site = site_ref[b, k]
                 chan = lax.div(site, cells)
                 cell = site - chan * cells
                 col = lax.rem(cell, LANES)
                 start = pl.multiple_of(cell - col, LANES)
-                block = ens_ref[chan, :, pl.ds(start, LANES)]
                 at = base + k
-                turned = pltpu.roll(block, lax.rem(at - col + LANES, LANES), 1)
-                acc = jnp.where(lane == at, turned, acc)
-            out_ref[:, spot] = acc
+                turn = lax.rem(at - col + LANES, LANES)
+                here = lane == at
+                for h in range(2):
+                    block = held_ref[2 * chan + h, :, pl.ds(start, LANES)]
+                    acc[h] = jnp.where(here, pltpu.roll(block, turn, 1), acc[h])
+            for h in range(2):
+                rows_ref[h * half:(h + 1) * half, spot] = acc[h]
 
         return carry
 
     lax.fori_loop(0, batches, one, 0)
-
-
-def gather_rows(ens, obs_site, owner_tile, batch_order, tile):
+    end.wait()
+    out.wait()
+
+
+def gather_rows(units, obs_site, owner_tile, batch_order, head, tail):
     batches, obs = obs_site.shape
+    count, half, cells = units.shape
+    f32 = jnp.float32
     return pl.pallas_call(
         gather_kernel,
-        out_shape=jax.ShapeDtypeStruct((ens.shape[1], batches * obs), jnp.float32),
-        in_specs=[SMEM, SMEM, SMEM, SMEM, VMEM],
-        out_specs=VMEM,
+        out_shape=(
+            pltpu.VMEM((2 * half, batches * obs), f32),
+            pltpu.HBM((count - head - tail, half, cells), f32),
+            pltpu.VMEM((tail, half, cells), f32),
+        ),
+        in_specs=[ANY] * 4,
+        out_specs=(VMEM, ANY, VMEM),
+        scratch_shapes=[
+            pltpu.VMEM(units.shape, f32),
+            pltpu.SMEM(obs_site.shape, jnp.int32),
+            pltpu.SMEM(owner_tile.shape, jnp.int32),
+            pltpu.SMEM(batch_order.shape, jnp.int32),
+            pltpu.SemaphoreType.DMA((6,)),
+        ],
+        compiler_params=pltpu.CompilerParams(vmem_limit_bytes=8 << 20),
         name="gather_rows",
-    )(obs_site, owner_tile, batch_order, tile, ens)
+    )(hbm(obs_site), hbm(owner_tile), hbm(batch_order), hbm(units))
 
 
 def spread(row):
     return jnp.broadcast_to(row, (SUBS, row.shape[1]))
 
 
-def chain_kernel(order_ref, owner_ref, mask_ref, var_ref, tile_ref, own_ref, oth_ref, val_ref,
+def chain_kernel(order_ref, owner_ref, mask_ref, var_ref, tile_ref, raw_ref, val_ref,
                  out_ref, w_ref, left_ref, right_ref, z_ref, v_ref, val_s):
     batches, obs = val_ref.shape
-    half = own_ref.shape[0]
-    members = 2 * half
+    members = raw_ref.shape[0]
+    half = members // 2
     total = batches * obs
     tiles = total // LANES
     per = LANES // obs
@@ -92,7 +155,7 @@
         values.append(row)
     values = jnp.concatenate(values, axis=1)
 
-    raw = jnp.concatenate([own_ref[...], oth_ref[...]], axis=0)
+    raw = raw_ref[...]
     mean = jnp.sum(raw, axis=0, keepdims=True) * (1.0 / members)
     anom = raw - mean
     first = lax.broadcasted_iota(jnp.int32, (SUBS, total), 0) == 0
@@ -189,15 +252,16 @@
     out_ref[...] = moved[members:members + half, :members]
 
 
-def chain(own, oth, obs_value, obs_var, owner_tile, tile_mask, batch_order, tile):
-    half, total = own.shape
+def chain(rows, obs_value, obs_var, owner_tile, tile_mask, batch_order, tile):
+    members, total = rows.shape
+    half = members // 2
     obs = obs_value.shape[1]
     width = total // LANES + 2
     f32 = jnp.float32
     return pl.pallas_call(
         chain_kernel,
-        out_shape=jax.ShapeDtypeStruct((half, 2 * half), f32),
-        in_specs=[SMEM] * 5 + [VMEM] * 3,
+        out_shape=pltpu.VMEM((half, members), f32),
+        in_specs=[SMEM] * 5 + [VMEM] * 2,
         out_specs=VMEM,
         scratch_shapes=[
             pltpu.VMEM((width, total, LANES), f32),
@@ -207,36 +271,88 @@
             pltpu.VMEM((total, LANES), f32),
             pltpu.VMEM((obs_value.shape[0], LANES), f32),
         ],
+        compiler_params=pltpu.CompilerParams(vmem_limit_bytes=8 << 20),
         name="chain",
-    )(batch_order, owner_tile, tile_mask, obs_var, tile, own, oth, obs_value)
-
-
-def apply_kernel(mat_ref, own_ref, oth_ref, out_ref):
-    half = mat_ref.shape[0]
-    mat = mat_ref[...]
+    )(batch_order, owner_tile, tile_mask, obs_var, tile, vmem(rows), obs_value)
+
+
+def left_factor(mat):
     high = mat.astype(jnp.bfloat16)
     low = (mat - high.astype(jnp.float32)).astype(jnp.bfloat16)
-    left = jnp.concatenate(
+    return jnp.concatenate(
         [jnp.concatenate([high, high], axis=1), jnp.concatenate([low, jnp.zeros_like(low)], axis=1)], axis=0)
-    own = own_ref[0]
-    x = jnp.concatenate([own, oth_ref[0]], axis=0)
+
+
+def apply_block(left, own, upper, lower):
+    half = own.shape[0]
+    x = jnp.concatenate([own, upper, lower], axis=0)
     x_high = x.astype(jnp.bfloat16)
     x_low = (x - x_high.astype(jnp.float32)).astype(jnp.bfloat16)
     y = jnp.dot(left, jnp.concatenate([x_high, x_low], axis=0), preferred_element_type=jnp.float32)
-    out_ref[0] = own + (y[:half] + y[half:])
-
-
-def apply_matrix(mat, own, oth):
-    chans, half, cells = own.shape
-    spec = pl.BlockSpec((1, half, cells), lambda c: (c, 0, 0))
+    return own + (y[:half] + y[half:])
+
+
+def apply_main(mat_ref, first_ref, main_ref, ens_hbm, out_hbm, own_ref, new_ref, sem_in, sem_out):
+    chans = own_ref.shape[0]
+    ahead = first_ref.shape[0]
+    loads = [pltpu.make_async_copy(ens_hbm.at[c], own_ref.at[c], sem_in.at[c]) for c in range(chans)]
+    stores = [pltpu.make_async_copy(new_ref.at[c], out_hbm.at[c], sem_out.at[c]) for c in range(chans)]
+    for load in loads:
+        load.start()
+    left = left_factor(mat_ref[...])
+    for c in range(chans):
+        oth = [first_ref[u] if u < ahead else main_ref[u - ahead] for u in (2 * c, 2 * c + 1)]
+        loads[c].wait()
+        new_ref[c] = apply_block(left, own_ref[c], *oth)
+        stores[c].start()
+    for store in stores:
+        store.wait()
+
+
+def apply_last(mat_ref, own_ref, last_ref, prev_hbm, out_hbm, new_ref, sem_out):
+    chans = new_ref.shape[0]
+    start = out_hbm.shape[0] - chans
+    stores = [pltpu.make_async_copy(new_ref.at[c], out_hbm.at[start + c], sem_out.at[c]) for c in range(chans)]
+    left = left_factor(mat_ref[...])
+    for c in range(chans):
+        own = jnp.concatenate([own_ref[2 * c], own_ref[2 * c + 1]], axis=0)
+        new_ref[c] = apply_block(left, own, last_ref[2 * c], last_ref[2 * c + 1])
+        stores[c].start()
+    for store in stores:
+        store.wait()
+
+
+def apply_matrix(mat, ens, first, main, own_last, last):
+    chans, half, cells = ens.shape
+    tail = last.shape[0] // 2
+    head = chans - tail
+    f32 = jnp.float32
+    state = pltpu.HBM(ens.shape, f32)
+    params = pltpu.CompilerParams(vmem_limit_bytes=8 << 20)
+    out = pl.pallas_call(
+        apply_main,
+        out_shape=state,
+        in_specs=[VMEM, VMEM, VMEM, ANY],
+        out_specs=ANY,
+        scratch_shapes=[
+            pltpu.VMEM((head, half, cells), f32),
+            pltpu.VMEM((head, half, cells), f32),
+            pltpu.SemaphoreType.DMA((head,)),
+            pltpu.SemaphoreType.DMA((head,)),
+        ],
+        compiler_params=params,
+        name="apply_main",
+    )(vmem(mat), vmem(first), vmem(main), hbm(ens))
     return pl.pallas_call(
-        apply_kernel,
-        grid=(chans,),
-        out_shape=jax.ShapeDtypeStruct(own.shape, jnp.float32),
-        in_specs=[pl.BlockSpec(mat.shape, lambda c: (0, 0)), spec, spec],
-        out_specs=spec,
-        name="apply",
-    )(mat, own, oth)
+        apply_last,
+        out_shape=state,
+        in_specs=[VMEM, VMEM, VMEM, ANY],
+        out_specs=ANY,
+        input_output_aliases={3: 0},
+        scratch_shapes=[pltpu.VMEM((tail, half, cells), f32), pltpu.SemaphoreType.DMA((tail,))],
+        compiler_params=params,
+        name="apply_last",
+    )(vmem(mat), vmem(own_last), vmem(last), hbm(out))
 
 
 def body(ensemble, obs_site, obs_value, obs_var, owner_tile, tile_mask, batch_order):
@@ -244,18 +360,21 @@
     n_tile = lax.axis_size("tile")
     swap = [(0, 1), (1, 0)]
     ens = jnp.transpose(ensemble, (1, 0, 2))
-    own = gather_rows(ens, obs_site, owner_tile, batch_order, tile)
+    chans, half, cells = ens.shape
+    units = ens.reshape(2 * chans, half // 2, cells)
+    head, tail = 1, 2
+    first = lax.ppermute(first_units(units, head), "mem", swap)
+    own, own_main, own_last = gather_rows(units, obs_site, owner_tile, batch_order, head, tail)
     oth = lax.ppermute(own, "mem", swap)
-    held, _ = lax.optimization_barrier((ens, own))
-    bulk = lax.ppermute(held, "mem", swap)
+    main = lax.ppermute(own_main, "mem", swap)
+    last = lax.ppermute(own_last, "mem", swap)
     rows = jnp.concatenate([own, oth], axis=0)
     step = 1
     while step < n_tile:
         rows = rows + lax.ppermute(rows, "tile", [(i, i ^ step) for i in range(n_tile)])
         step *= 2
-    half = own.shape[0]
-    mat = chain(rows[:half], rows[half:], obs_value, obs_var, owner_tile, tile_mask, batch_order, tile)
-    out = apply_matrix(mat, ens, bulk)
+    mat = chain(rows, obs_value, obs_var, owner_tile, tile_mask, batch_order, tile)
+    out = apply_matrix(mat, ens, first, main, own_last, last)
     return jnp.transpose(out, (1, 0, 2))
 
 

time: 85.8 us -> 73.1 us (0.85)
  waiting for transfers between devices: 48.3 us -> 38.3 us
  Pallas kernels: 24.8 us -> 22.3 us
  starting transfers between devices: 10.2 us -> 12 us
  other arithmetic: 1.56 us -> 0.04 us
    ppermute x1, waiting for transfers between devices: 40 us -> 32.4 us  [body(): oth = lax.ppermute(own, 'mem', swap)]
    ppermute x1 -> x3, starting transfers between devices: 3 us -> 6.11 us  [the longest x1 3.06 us: body(): main = lax.ppermute(own_main, 'mem', swap)]
    pallas_call x3 -> x5, Pallas kernels: 24.8 us -> 22.3 us  [the longest x1 14.6 us: chain(): pl.pallas_call(chain_kernel, out_shape=pltpu.VMEM((half, members), f32),...]
    ppermute x4, waiting for transfers between devices: 8.22 us -> 5.87 us  [body(): lax.ppermute(rows, 'tile', [(i, i ^ step) for i in range(n_tile)])]
    ppermute x4, starting transfers between devices: 7.14 us -> 5.85 us  [body(): lax.ppermute(rows, 'tile', [(i, i ^ step) for i in range(n_tile)])]
  transfers between devices with their start and end apart: 6 -> 8, of which waited for: 5 -> 4; matrix products, arithmetic and copies ran while one was open for 3% -> 0% of each run, Pallas kernels for 18% -> 26%
where the time goes in v3:
time: 73.1 us; the launch traced here: 72.9 us
  waiting for transfers between devices  38.3 us (52%)
  Pallas kernels  22.3 us (31%)
  starting transfers between devices  12 us (16%)
    ppermute x1, waiting for transfers between devices, body(): oth = lax.ppermute(own, 'mem', swap)  32.4 us
    pallas_call x1, Pallas kernels, chain(): pl.pallas_call(chain_kernel, out_shape=pltpu.VMEM((half, members), f32),...  14.6 us
    ppermute x4, waiting for transfers between devices, body(): lax.ppermute(rows, 'tile', [(i, i ^ step) for i in range(n_tile)])  5.87 us
    ppermute x4, starting transfers between devices, body(): lax.ppermute(rows, 'tile', [(i, i ^ step) for i in range(n_tile)])  5.85 us
    pallas_call x1, Pallas kernels, apply_matrix(): pl.pallas_call(apply_main, out_shape=state, in_specs=[VMEM, VMEM, VMEM, A...  3.2 us
    ppermute x1, starting transfers between devices, body(): main = lax.ppermute(own_main, 'mem', swap)  3.06 us
    pallas_call x1, Pallas kernels, gather_rows(): pl.pallas_call(gather_kernel, out_shape=(pltpu.VMEM((2 * half, batches *...  2.65 us
    ppermute x1, starting transfers between devices, body(): last = lax.ppermute(own_last, 'mem', swap)  1.8 us
  transfers between devices with their start and end apart: 8, of which 4 were waited for; matrix products, arithmetic and copies ran while one was open for 0% of the time, Pallas kernels for 26%

profile of v3, /device:TPU:0, one launch (start us, length us, event | category | flops | bytes accessed | tf_op | source)
XLA Modules:
  0.0 72.9 jit_solution(1739375105959284166)
XLA Ops:
  0.0 2.7 %gather_rows.1 = (f32[32,256]{1,0:T(8,128)S(1)}, f32[11,16,2048]{2,1,0:T(8,128)}, f32[2,16,2048]{2,1,0:T(8,128)S(1)}) custom-call(s32[8,32]{1,0:T(8,128)} %site_hbm.1, s32[8]{0:T(128)} %owner_ref.1, s32[8]{0:T(128)} %order_ref.1, f32[14,16,2048]{2,1,0:T(8,128)} %bitcast.5), custom_call_target="tpu_custom_call" | custom-call | tf_op jit(solution)/shard_map/gather_rows/pallas_call | solution.py:102
  2.7 0.0 copy-start
  2.7 0.0 copy-start.1
  2.7 0.0 copy-start.2
  2.7 0.0 copy-start.3
  2.7 0.0 copy-start.4
  2.7 3.1 %collective-permute-start.7 = (f32[11,16,2048]{2,1,0:T(8,128)}, f32[11,16,2048]{2,1,0:T(8,128)S(1)}, u32[]{:S(2)}, u32[]{:S(2)}) collective-permute-start(f32[11,16,2048]{2,1,0:T(8,128)} %get-tuple-element.10), channel_id=1, source_target_pairs={{0,1},{1,0},{2,3},{3,2},{4,5},{5,4},{6,7},{7,6},{8,9},{9,8},{10,11... | collective-permute-start | bytes 4325384 | tf_op jit(solution)/shard_map/ppermute | solution.py:369
  5.8 0.1 collective-permute-start
  5.9 32.4 %collective-permute-done = f32[32,256]{1,0:T(8,128)S(1)} collective-permute-done((f32[32,256]{1,0:T(8,128)S(1)}, f32[32,256]{1,0:T(8,128)S(1)}, u32[]{:S(2)}, u32[]{:S(2)}) %collective-permute-start) | collective-permute-done | bytes 32800 | tf_op jit(solution)/shard_map/ppermute | solution.py:368
  38.3 0.0 collective-permute-start.1
  38.3 1.8 %collective-permute-start.5 = (f32[2,16,2048]{2,1,0:T(8,128)S(1)}, f32[2,16,2048]{2,1,0:T(8,128)S(1)}, u32[]{:S(2)}, u32[]{:S(2)}) collective-permute-start(f32[2,16,2048]{2,1,0:T(8,128)S(1)} %get-tuple-element.9.own_ref), channel_id=1, source_target_pairs={{0,1},{1,0},{2,3},{3,2},{4,5},{5,4},{6,7},{7,6},{8,9},{9,8},{10,11... | collective-permute-start | bytes 786440 | tf_op jit(solution)/shard_map/ppermute | solution.py:370
  40.1 0.0 collective-permute-done.1
  40.1 1.6 %collective-permute-start.2 = (f32[64,256]{1,0:T(8,128)S(1)}, f32[64,256]{1,0:T(8,128)S(1)}, u32[]{:S(2)}, u32[]{:S(2)}) collective-permute-start(f32[64,256]{1,0:T(8,128)S(1)} %add.12), channel_id=1, source_target_pairs={{0,4},{2,6},{4,0},{6,2},{8,12},{10,14},{12,8},{14,10},{16,20},{18,... | collective-permute-start | bytes 196616 | tf_op jit(solution)/shard_map/ppermute | solution.py:374
  41.7 2.8 %collective-permute-done.2 = f32[64,256]{1,0:T(8,128)S(1)} collective-permute-done((f32[64,256]{1,0:T(8,128)S(1)}, f32[64,256]{1,0:T(8,128)S(1)}, u32[]{:S(2)}, u32[]{:S(2)}) %collective-permute-start.2) | collective-permute-done | bytes 65568 | tf_op jit(solution)/shard_map/ppermute | solution.py:374
  44.4 1.6 %collective-permute-start.3 = (f32[64,256]{1,0:T(8,128)S(1)}, f32[64,256]{1,0:T(8,128)S(1)}, u32[]{:S(2)}, u32[]{:S(2)}) collective-permute-start(f32[64,256]{1,0:T(8,128)S(1)} %add.13), channel_id=1, source_target_pairs={{0,8},{2,10},{4,12},{6,14},{8,0},{10,2},{12,4},{14,6},{16,24},{18,... | collective-permute-start | bytes 196616 | tf_op jit(solution)/shard_map/ppermute | solution.py:374
  46.1 0.9 %first_units.1 = f32[1,16,2048]{2,1,0:T(8,128)S(1)} custom-call(f32[14,16,2048]{2,1,0:T(8,128)} %bitcast.6), custom_call_target="tpu_custom_call" | custom-call | tf_op jit(solution)/shard_map/first_units/pallas_call | solution.py:33
  47.0 1.3 %collective-permute-start.6 = (f32[1,16,2048]{2,1,0:T(8,128)S(1)}, f32[1,16,2048]{2,1,0:T(8,128)S(1)}, u32[]{:S(2)}, u32[]{:S(2)}) collective-permute-start(f32[1,16,2048]{2,1,0:T(8,128)S(1)} %first_units.1), channel_id=1, source_target_pairs={{0,1},{1,0},{2,3},{3,2},{4,5},{5,4},{6,7},{7,6},{8,9},{9,8},{10,11... | collective-permute-start | bytes 393224 | tf_op jit(solution)/shard_map/ppermute | solution.py:366
  48.3 0.5 collective-permute-done.3
  48.8 2.7 %collective-permute-start.4 = (f32[64,256]{1,0:T(8,128)S(1)}, f32[64,256]{1,0:T(8,128)S(1)}, u32[]{:S(2)}, u32[]{:S(2)}) collective-permute-start(f32[64,256]{1,0:T(8,128)S(1)} %add.14), channel_id=1, source_target_pairs={{0,16},{2,18},{4,20},{6,22},{8,24},{10,26},{12,28},{14,30},{16,0},... | collective-permute-start | bytes 196616 | tf_op jit(solution)/shard_map/ppermute | solution.py:374
  51.4 2.6 %collective-permute-done.4 = f32[64,256]{1,0:T(8,128)S(1)} collective-permute-done((f32[64,256]{1,0:T(8,128)S(1)}, f32[64,256]{1,0:T(8,128)S(1)}, u32[]{:S(2)}, u32[]{:S(2)}) %collective-permute-start.4) | collective-permute-done | bytes 65568 | tf_op jit(solution)/shard_map/ppermute | solution.py:374
  54.0 0.0 copy-done
  54.0 0.0 copy-done.1
  54.1 0.0 copy-done.2
  54.1 0.0 copy-done.3
  54.1 0.0 copy-done.4
  54.1 14.6 %chain.1.mat_ref = f32[32,64]{1,0:T(8,128)S(1)} custom-call(s32[8]{0:T(128)S(1)} %copy-done.3, s32[8]{0:T(128)S(1)} %copy-done.4, s32[8,16]{1,0:T(8,128)S(1)} %copy-done, f32[8,32]{1,0:T(8,128)S(1)} %copy-done.1, s32[1]{0:T(128)} %bitcast.tile_ref, f32[64,256]{1,0:T(8,128)S(1)} %add.15.raw_ref, f32[8,32]{1,0:T(8,128)S(1)} %copy-done.2), custom_call_target="tpu_custom_call" | custom-call | tf_op jit(solution)/shard_map/chain/pallas_call | solution.py:261
  68.7 0.0 collective-permute-done.6.first_ref
  68.7 0.0 collective-permute-done.7.main_ref
  68.7 3.2 %apply_main.1.prev_hbm = f32[7,32,2048]{2,1,0:T(8,128)} custom-call(f32[32,64]{1,0:T(8,128)S(1)} %chain.1.mat_ref, f32[1,16,2048]{2,1,0:T(8,128)S(1)} %collective-permute-done.6.first_ref, f32[11,16,2048]{2,1,0:T(8,128)S(1)} %collective-permute-done.7.main_ref, f32[7,32,2048]{2,1,0:T(8,128)} %bitcast.7), custom_call_target="tpu_custom_call" | custom-call | tf_op jit(solution)/shard_map/apply_main/pallas_call | solution.py:332
  71.9 0.0 collective-permute-done.5.last_ref
  71.9 1.0 %apply_last.1 = f32[7,32,2048]{2,1,0:T(8,128)} custom-call(f32[32,64]{1,0:T(8,128)S(1)} %chain.1.mat_ref, f32[2,16,2048]{2,1,0:T(8,128)S(1)} %get-tuple-element.9.own_ref, f32[2,16,2048]{2,1,0:T(8,128)S(1)} %collective-permute-done.5.last_ref, f32[7,32,2048]{2,1,0:T(8,128)} %apply_main.1.prev_hbm), custom_call_target="tpu_custom_call", output_to_operand_aliasing={{}: (3, {})} | custom-call | tf_op jit(solution)/shard_map/apply_last/pallas_call | solution.py:346
  (6 shorter events, 0.0 us)
Async XLA Ops:
  2.7 51.4 %copy-start = (s32[8,16]{1,0:T(8,128)S(1)}, s32[8,16]{1,0:T(8,128)}, u32[]{:S(2)}) copy-start(s32[8,16]{1,0:T(8,128)} %mask_ref.1) | copy-start | bytes 1540
  2.7 51.4 %copy-start.1 = (f32[8,32]{1,0:T(8,128)S(1)}, f32[8,32]{1,0:T(8,128)}, u32[]{:S(2)}) copy-start(f32[8,32]{1,0:T(8,128)} %var_ref.1) | copy-start | bytes 3076
  2.7 51.4 %copy-start.2 = (f32[8,32]{1,0:T(8,128)S(1)}, f32[8,32]{1,0:T(8,128)}, u32[]{:S(2)}) copy-start(f32[8,32]{1,0:T(8,128)} %val_ref.1) | copy-start | bytes 3076
  2.7 51.4 %copy-start.3 = (s32[8]{0:T(128)S(1)}, s32[8]{0:T(128)}, u32[]{:S(2)}) copy-start(s32[8]{0:T(128)} %order_ref.1) | copy-start | bytes 100
  2.7 51.4 %copy-start.4 = (s32[8]{0:T(128)S(1)}, s32[8]{0:T(128)}, u32[]{:S(2)}) copy-start(s32[8]{0:T(128)} %owner_ref.1) | copy-start | bytes 100
  2.7 66.0 %collective-permute-start.7 = (f32[11,16,2048]{2,1,0:T(8,128)}, f32[11,16,2048]{2,1,0:T(8,128)S(1)}, u32[]{:S(2)}, u32[]{:S(2)}) collective-permute-start(f32[11,16,2048]{2,1,0:T(8,128)} %get-tuple-element.10), channel_id=1, source_target_pairs={{0,1},{1,0},{2,3},{3,2},{4,5},{5,4},{6,7},{7,6},{8,9},{9,8},{10,11... | collective-permute-start | bytes 4325384 | tf_op jit(solution)/shard_map/ppermute | solution.py:369
  5.8 32.5 %collective-permute-start = (f32[32,256]{1,0:T(8,128)S(1)}, f32[32,256]{1,0:T(8,128)S(1)}, u32[]{:S(2)}, u32[]{:S(2)}) collective-permute-start(f32[32,256]{1,0:T(8,128)S(1)} %get-tuple-element.8), channel_id=1, source_target_pairs={{0,1},{1,0},{2,3},{3,2},{4,5},{5,4},{6,7},{7,6},{8,9},{9,8},{10,11... | collective-permute-start | bytes 98312 | tf_op jit(solution)/shard_map/ppermute | solution.py:368
  38.3 1.8 %collective-permute-start.1 = (f32[64,256]{1,0:T(8,128)S(1)}, f32[64,256]{1,0:T(8,128)S(1)}, u32[]{:S(2)}, u32[]{:S(2)}) collective-permute-start(f32[64,256]{1,0:T(8,128)S(1)} %constant_dynamic-update-slice_fusion), channel_id=1, source_target_pairs={{0,2},{2,0},{4,6},{6,4},{8,10},{10,8},{12,14},{14,12},{16,18},{18,... | collective-permute-start | bytes 196616 | tf_op jit(solution)/shard_map/ppermute | solution.py:374
  38.3 33.6 %collective-permute-start.5 = (f32[2,16,2048]{2,1,0:T(8,128)S(1)}, f32[2,16,2048]{2,1,0:T(8,128)S(1)}, u32[]{:S(2)}, u32[]{:S(2)}) collective-permute-start(f32[2,16,2048]{2,1,0:T(8,128)S(1)} %get-tuple-element.9.own_ref), channel_id=1, source_target_pairs={{0,1},{1,0},{2,3},{3,2},{4,5},{5,4},{6,7},{7,6},{8,9},{9,8},{10,11... | collective-permute-start | bytes 786440 | tf_op jit(solution)/shard_map/ppermute | solution.py:370
  40.1 4.3 %collective-permute-start.2 = (f32[64,256]{1,0:T(8,128)S(1)}, f32[64,256]{1,0:T(8,128)S(1)}, u32[]{:S(2)}, u32[]{:S(2)}) collective-permute-start(f32[64,256]{1,0:T(8,128)S(1)} %add.12), channel_id=1, source_target_pairs={{0,4},{2,6},{4,0},{6,2},{8,12},{10,14},{12,8},{14,10},{16,20},{18,... | collective-permute-start | bytes 196616 | tf_op jit(solution)/shard_map/ppermute | solution.py:374
  44.4 4.3 %collective-permute-start.3 = (f32[64,256]{1,0:T(8,128)S(1)}, f32[64,256]{1,0:T(8,128)S(1)}, u32[]{:S(2)}, u32[]{:S(2)}) collective-permute-start(f32[64,256]{1,0:T(8,128)S(1)} %add.13), channel_id=1, source_target_pairs={{0,8},{2,10},{4,12},{6,14},{8,0},{10,2},{12,4},{14,6},{16,24},{18,... | collective-permute-start | bytes 196616 | tf_op jit(solution)/shard_map/ppermute | solution.py:374
  47.0 21.7 %collective-permute-start.6 = (f32[1,16,2048]{2,1,0:T(8,128)S(1)}, f32[1,16,2048]{2,1,0:T(8,128)S(1)}, u32[]{:S(2)}, u32[]{:S(2)}) collective-permute-start(f32[1,16,2048]{2,1,0:T(8,128)S(1)} %first_units.1), channel_id=1, source_target_pairs={{0,1},{1,0},{2,3},{3,2},{4,5},{5,4},{6,7},{7,6},{8,9},{9,8},{10,11... | collective-permute-start | bytes 393224 | tf_op jit(solution)/shard_map/ppermute | solution.py:366
  48.8 5.2 %collective-permute-start.4 = (f32[64,256]{1,0:T(8,128)S(1)}, f32[64,256]{1,0:T(8,128)S(1)}, u32[]{:S(2)}, u32[]{:S(2)}) collective-permute-start(f32[64,256]{1,0:T(8,128)S(1)} %add.14), channel_id=1, source_target_pairs={{0,16},{2,18},{4,20},{6,22},{8,24},{10,26},{12,28},{14,30},{16,0},... | collective-permute-start | bytes 196616 | tf_op jit(solution)/shard_map/ppermute | solution.py:374

commit v4 on v3

--- a/solution.py
+++ b/solution.py
@@ -40,29 +40,32 @@
     )(hbm(units))
 
 
-def gather_kernel(site_hbm, owner_hbm, order_hbm, units_hbm, rows_ref, main_hbm, last_ref,
-                  held_ref, site_ref, owner_ref, order_ref, sem):
+def split(value, size):
+    if size & (size - 1) == 0:
+        return lax.shift_right_logical(value, size.bit_length() - 1), lax.bitwise_and(value, size - 1)
+    quotient = lax.div(value, size)
+    return quotient, value - quotient * size
+
+
+def gather_kernel(site_hbm, owner_hbm, order_hbm, units_hbm, first_ref, rows_ref, main_ref, last_ref,
+                  site_ref, owner_ref, order_ref, sem):
     batches, obs = site_hbm.shape
     count, half, cells = units_hbm.shape
     per = LANES // obs
-    tail = last_ref.shape[0]
-    middle = main_hbm.shape[0]
-    state = pltpu.make_async_copy(units_hbm, held_ref, sem.at[0])
-    small = [
-        pltpu.make_async_copy(site_hbm, site_ref, sem.at[1]),
-        pltpu.make_async_copy(owner_hbm, owner_ref, sem.at[2]),
-        pltpu.make_async_copy(order_hbm, order_ref, sem.at[3]),
+    head, middle, tail = first_ref.shape[0], main_ref.shape[0], last_ref.shape[0]
+    copies = [
+        pltpu.make_async_copy(owner_hbm, owner_ref, sem.at[0]),
+        pltpu.make_async_copy(order_hbm, order_ref, sem.at[1]),
+        pltpu.make_async_copy(site_hbm, site_ref, sem.at[2]),
+        pltpu.make_async_copy(units_hbm.at[pl.ds(head, middle)], main_ref, sem.at[3]),
+        pltpu.make_async_copy(units_hbm.at[pl.ds(count - tail, tail)], last_ref, sem.at[4]),
     ]
-    end = pltpu.make_async_copy(units_hbm.at[pl.ds(count - tail, tail)], last_ref, sem.at[4])
-    for copy in small + [state, end]:
+    for copy in copies:
         copy.start()
     tile = lax.axis_index("tile")
     lane = lax.broadcasted_iota(jnp.int32, (half, LANES), 1)
     rows_ref[...] = jnp.zeros_like(rows_ref)
-    state.wait()
-    out = pltpu.make_async_copy(held_ref.at[pl.ds(count - tail - middle, middle)], main_hbm, sem.at[5])
-    out.start()
-    for copy in small:
+    for copy in copies:
         copy.wait()
 
     def one(p, carry):
@@ -70,32 +73,33 @@
 
         @pl.when(owner_ref[b] == tile)
         def _():
-            base = lax.rem(p, per) * obs
-            spot = pl.ds(pl.multiple_of(lax.div(p, per) * LANES, LANES), LANES)
+            group, place = split(p, per)
+            base = place * obs
+            spot = pl.ds(pl.multiple_of(group * LANES, LANES), LANES)
             acc = [rows_ref[h * half:(h + 1) * half, spot] for h in range(2)]
             for k in range(obs):
-                site = site_ref[b, k]
-                chan = lax.div(site, cells)
-                cell = site - chan * cells
-                col = lax.rem(cell, LANES)
-                start = pl.multiple_of(cell - col, LANES)
+                chan, cell = split(site_ref[b, k], cells)
+                _, col = split(cell, LANES)
+                here = pl.ds(pl.multiple_of(cell - col, LANES), LANES)
                 at = base + k
-                turn = lax.rem(at - col + LANES, LANES)
-                here = lane == at
+                turn = lax.bitwise_and(at - col, LANES - 1)
+                mine = lane == at
                 for h in range(2):
-                    block = held_ref[2 * chan + h, :, pl.ds(start, LANES)]
-                    acc[h] = jnp.where(here, pltpu.roll(block, turn, 1), acc[h])
+                    unit = 2 * chan + h
+                    block = main_ref[jnp.clip(unit - head, 0, middle - 1), :, here]
+                    early = first_ref[jnp.minimum(unit, head - 1), :, here]
+                    late = last_ref[jnp.clip(unit - (count - tail), 0, tail - 1), :, here]
+                    block = jnp.where(unit < head, early, jnp.where(unit >= count - tail, late, block))
+                    acc[h] = jnp.where(mine, pltpu.roll(block, turn, 1), acc[h])
             for h in range(2):
                 rows_ref[h * half:(h + 1) * half, spot] = acc[h]
 
         return carry
 
     lax.fori_loop(0, batches, one, 0)
-    end.wait()
-    out.wait()
-
-
-def gather_rows(units, obs_site, owner_tile, batch_order, head, tail):
+
+
+def gather_rows(units, first, obs_site, owner_tile, batch_order, tail):
     batches, obs = obs_site.shape
     count, half, cells = units.shape
     f32 = jnp.float32
@@ -103,25 +107,31 @@
         gather_kernel,
         out_shape=(
             pltpu.VMEM((2 * half, batches * obs), f32),
-            pltpu.HBM((count - head - tail, half, cells), f32),
+            pltpu.VMEM((count - first.shape[0] - tail, half, cells), f32),
             pltpu.VMEM((tail, half, cells), f32),
         ),
-        in_specs=[ANY] * 4,
-        out_specs=(VMEM, ANY, VMEM),
+        in_specs=[ANY] * 4 + [VMEM],
+        out_specs=(VMEM, VMEM, VMEM),
         scratch_shapes=[
-            pltpu.VMEM(units.shape, f32),
             pltpu.SMEM(obs_site.shape, jnp.int32),
             pltpu.SMEM(owner_tile.shape, jnp.int32),
             pltpu.SMEM(batch_order.shape, jnp.int32),
-            pltpu.SemaphoreType.DMA((6,)),
+            pltpu.SemaphoreType.DMA((5,)),
         ],
         compiler_params=pltpu.CompilerParams(vmem_limit_bytes=8 << 20),
         name="gather_rows",
-    )(hbm(obs_site), hbm(owner_tile), hbm(batch_order), hbm(units))
+    )(hbm(obs_site), hbm(owner_tile), hbm(batch_order), hbm(units), vmem(first))
 
 
 def spread(row):
     return jnp.broadcast_to(row, (SUBS, row.shape[1]))
+
+
+def left_factor(mat):
+    high = mat.astype(jnp.bfloat16)
+    low = (mat - high.astype(jnp.float32)).astype(jnp.bfloat16)
+    return jnp.concatenate(
+        [jnp.concatenate([high, high], axis=1), jnp.concatenate([low, jnp.zeros_like(low)], axis=1)], axis=0)
 
 
 def chain_kernel(order_ref, owner_ref, mask_ref, var_ref, tile_ref, raw_ref, val_ref,
@@ -199,57 +209,68 @@
         wp = [[w_ref[t, pl.ds(pl.multiple_of(start + i * SUBS, SUBS), SUBS), :] for i in range(blocks)]
               for t in range(width)]
         shift = lax.rem(LANES - lax.rem(p, per) * obs, LANES)
-        gram = w_ref[lax.div(p, per), rows, :]
+        gram = w_ref[lax.div(p, per), rows, :] * inv
         gram = pltpu.roll(gram, shift, 1)
         cols = [[jnp.broadcast_to(gram[i * SUBS:(i + 1) * SUBS, j:j + 1], (SUBS, LANES)) if i >= j // SUBS else None
                  for i in range(blocks)] for j in range(obs)]
-        for k in range(obs):
+        for k in range(0, obs, 2):
             kb, ks = k // SUBS, k % SUBS
-            col = cols[k]
-            var = var_ref[b, k]
-            pivot = spread(col[kb][ks:ks + 1, :])
-            g = 1.0 / (pivot * inv + var)
-            weight = g * inv
-            beta = weight / (1.0 + jnp.sqrt(var * g))
-            below = [None] * blocks
-            below[kb] = jnp.where(sub8 > ks, col[kb], 0.0)
-            for i in range(kb + 1, blocks):
-                below[i] = col[i]
-            for j in range(k + 1, obs):
+            one, two = cols[k], cols[k + 1]
+            var1, var2 = var_ref[b, k], var_ref[b, k + 1]
+            cross = spread(one[kb][ks + 1:ks + 2, :])
+            total1 = spread(one[kb][ks:ks + 1, :]) + var1
+            total2 = spread(two[kb][ks + 1:ks + 2, :]) + var2
+            g1 = 1.0 / total1
+            g2 = total1 * (1.0 / (total1 * total2 - cross * cross))
+            ratio = g1 * cross
+            for j in range(k + 2, obs):
                 jb, js = j // SUBS, j % SUBS
-                factor = weight * spread(col[jb][js:js + 1, :])
+                h1 = spread(one[jb][js:js + 1, :])
+                h2 = spread(two[jb][js:js + 1, :])
+                f2 = g2 * (h2 - ratio * h1)
+                f1 = g1 * h1 - ratio * f2
                 for i in range(jb, blocks):
-                    cols[j][i] = cols[j][i] - col[i] * factor
+                    cols[j][i] = cols[j][i] - (one[i] * f1 + two[i] * f2)
+            moved = [two[i] - one[i] * ratio if two[i] is not None else None for i in range(blocks)]
+            below1 = [None] * kb + [jnp.where(sub8 > ks, one[kb], 0.0)] + one[kb + 1:]
+            below2 = [None] * kb + [jnp.where(sub8 > ks + 1, moved[kb], 0.0)] + moved[kb + 1:]
+            beta1 = g1 / (1.0 + jnp.sqrt(var1 * g1))
+            beta2 = g2 / (1.0 + jnp.sqrt(var2 * g2))
             for t in range(width):
-                wk = spread(wp[t][kb][ks:ks + 1, :])
-                both = jnp.where(pick_w[t], weight, beta) * wk
-                single = jnp.where(pick_b[t], beta, 0.0) * wk
-                right_ref[k:k + 1, t * LANES:(t + 1) * LANES] = both[:1]
-                right_ref[obs + k:obs + k + 1, t * LANES:(t + 1) * LANES] = single[:1]
+                u1 = spread(wp[t][kb][ks:ks + 1, :])
+                both1 = jnp.where(pick_w[t], g1, beta1) * u1
+                u2 = spread(wp[t][kb][ks + 1:ks + 2, :]) - cross * both1
+                both2 = jnp.where(pick_w[t], g2, beta2) * u2
+                here = slice(t * LANES, (t + 1) * LANES)
+                right_ref[k:k + 1, here] = both1[:1]
+                right_ref[k + 1:k + 2, here] = both2[:1]
+                right_ref[obs + k:obs + k + 1, here] = (jnp.where(pick_b[t], beta1, 0.0) * u1)[:1]
+                right_ref[obs + k + 1:obs + k + 2, here] = (jnp.where(pick_b[t], beta2, 0.0) * u2)[:1]
                 for i in range(kb, blocks):
-                    wp[t][i] = wp[t][i] - below[i] * both
+                    wp[t][i] = wp[t][i] - (below1[i] * both1 + below2[i] * both2)
         for t in range(tiles):
             for i in range(blocks):
-                d = wp[t][i] * late[t]
+                d = wp[t][i] * (late[t] * inv)
                 left_ref[i * SUBS:(i + 1) * SUBS, t * LANES:(t + 1) * LANES] = d * act[t]
                 left_ref[obs + i * SUBS:obs + (i + 1) * SUBS, t * LANES:(t + 1) * LANES] = d * (1.0 - act[t])
         for i in range(blocks):
             at = pl.ds(pl.multiple_of(start + i * SUBS, SUBS), SUBS)
             z_ref[at, :] = wp[tiles][i] * mine_f
         gain = jnp.broadcast_to(right_ref[:obs, (width - 1) * LANES:(width - 1) * LANES + 1], (obs, LANES))
-        v_ref[rows, :] = gain - right_ref[:obs, tiles * LANES:(tiles + 1) * LANES]
-
-        @pl.when(p < batches - 1)
-        def _():
-            update = contract(left_ref[...], right_ref[...])
-            for t in range(width):
-                w_ref[t] = w_ref[t] - update[:, t * LANES:(t + 1) * LANES]
+        v_ref[rows, :] = (gain - right_ref[:obs, tiles * LANES:(tiles + 1) * LANES]) * inv
+
+        for low in range(tiles):
+            @pl.when((p < batches - 1) & (lax.div(p + 1, per) == low))
+            def _():
+                update = contract(left_ref[:, low * LANES:], right_ref[:, low * LANES:])
+                for t in range(low, width):
+                    w_ref[t, low * LANES:, :] = w_ref[t, low * LANES:, :] - update[:, (t - low) * LANES:(t - low + 1) * LANES]
 
         return carry
 
     lax.fori_loop(0, batches, batch, 0)
     moved = contract(v_ref[...], z_ref[...])
-    out_ref[...] = moved[members:members + half, :members]
+    out_ref[...] = left_factor(moved[members:members + half, :members])
 
 
 def chain(rows, obs_value, obs_var, owner_tile, tile_mask, batch_order, tile):
@@ -260,7 +281,7 @@
     f32 = jnp.float32
     return pl.pallas_call(
         chain_kernel,
-        out_shape=pltpu.VMEM((half, members), f32),
+        out_shape=pltpu.VMEM((2 * half, 2 * members), jnp.bfloat16),
         in_specs=[SMEM] * 5 + [VMEM] * 2,
         out_specs=VMEM,
         scratch_shapes=[
@@ -276,13 +297,6 @@
     )(batch_order, owner_tile, tile_mask, obs_var, tile, vmem(rows), obs_value)
 
 
-def left_factor(mat):
-    high = mat.astype(jnp.bfloat16)
-    low = (mat - high.astype(jnp.float32)).astype(jnp.bfloat16)
-    return jnp.concatenate(
-        [jnp.concatenate([high, high], axis=1), jnp.concatenate([low, jnp.zeros_like(low)], axis=1)], axis=0)
-
-
 def apply_block(left, own, upper, lower):
     half = own.shape[0]
     x = jnp.concatenate([own, upper, lower], axis=0)
@@ -292,18 +306,27 @@
     return own + (y[:half] + y[half:])
 
 
-def apply_main(mat_ref, first_ref, main_ref, ens_hbm, out_hbm, own_ref, new_ref, sem_in, sem_out):
-    chans = own_ref.shape[0]
+def apply_main(mat_ref, own_first_ref, own_main_ref, first_ref, main_hbm, out_hbm, main_ref, new_ref, sem_in, sem_out):
+    chans = new_ref.shape[0]
     ahead = first_ref.shape[0]
-    loads = [pltpu.make_async_copy(ens_hbm.at[c], own_ref.at[c], sem_in.at[c]) for c in range(chans)]
     stores = [pltpu.make_async_copy(new_ref.at[c], out_hbm.at[c], sem_out.at[c]) for c in range(chans)]
-    for load in loads:
-        load.start()
-    left = left_factor(mat_ref[...])
+    loads = []
     for c in range(chans):
-        oth = [first_ref[u] if u < ahead else main_ref[u - ahead] for u in (2 * c, 2 * c + 1)]
-        loads[c].wait()
-        new_ref[c] = apply_block(left, own_ref[c], *oth)
+        low, high = max(2 * c - ahead, 0), max(2 * c + 2 - ahead, 0)
+        part = pl.ds(low, high - low)
+        loads.append(pltpu.make_async_copy(main_hbm.at[part], main_ref.at[part], sem_in.at[c]) if high > low else None)
+        if high > low:
+            loads[c].start()
+    left = mat_ref[...]
+
+    def pair(a, b, c):
+        return [a[u] if u < ahead else b[u - ahead] for u in (2 * c, 2 * c + 1)]
+
+    for c in range(chans):
+        own = jnp.concatenate(pair(own_first_ref, own_main_ref, c), axis=0)
+        if loads[c] is not None:
+            loads[c].wait()
+        new_ref[c] = apply_block(left, own, *pair(first_ref, main_ref, c))
         stores[c].start()
     for store in stores:
         store.wait()
@@ -313,7 +336,7 @@
     chans = new_ref.shape[0]
     start = out_hbm.shape[0] - chans
     stores = [pltpu.make_async_copy(new_ref.at[c], out_hbm.at[start + c], sem_out.at[c]) for c in range(chans)]
-    left = left_factor(mat_ref[...])
+    left = mat_ref[...]
     for c in range(chans):
         own = jnp.concatenate([own_ref[2 * c], own_ref[2 * c + 1]], axis=0)
         new_ref[c] = apply_block(left, own, last_ref[2 * c], last_ref[2 * c + 1])
@@ -322,27 +345,27 @@
         store.wait()
 
 
-def apply_matrix(mat, ens, first, main, own_last, last):
-    chans, half, cells = ens.shape
+def apply_matrix(mat, shape, own_first, own_main, own_last, first, main, last):
+    chans, half, cells = shape
     tail = last.shape[0] // 2
     head = chans - tail
     f32 = jnp.float32
-    state = pltpu.HBM(ens.shape, f32)
+    state = pltpu.HBM(shape, f32)
     params = pltpu.CompilerParams(vmem_limit_bytes=8 << 20)
     out = pl.pallas_call(
         apply_main,
         out_shape=state,
-        in_specs=[VMEM, VMEM, VMEM, ANY],
+        in_specs=[VMEM] * 4 + [ANY],
         out_specs=ANY,
         scratch_shapes=[
-            pltpu.VMEM((head, half, cells), f32),
+            pltpu.VMEM(main.shape, f32),
             pltpu.VMEM((head, half, cells), f32),
             pltpu.SemaphoreType.DMA((head,)),
             pltpu.SemaphoreType.DMA((head,)),
         ],
         compiler_params=params,
         name="apply_main",
-    )(vmem(mat), vmem(first), vmem(main), hbm(ens))
+    )(vmem(mat), vmem(own_first), vmem(own_main), vmem(first), hbm(main))
     return pl.pallas_call(
         apply_last,
         out_shape=state,
@@ -362,9 +385,10 @@
     ens = jnp.transpose(ensemble, (1, 0, 2))
     chans, half, cells = ens.shape
     units = ens.reshape(2 * chans, half // 2, cells)
-    head, tail = 1, 2
-    first = lax.ppermute(first_units(units, head), "mem", swap)
-    own, own_main, own_last = gather_rows(units, obs_site, owner_tile, batch_order, head, tail)
+    head, tail = 2, 2
+    own_first = first_units(units, head)
+    first = lax.ppermute(own_first, "mem", swap)
+    own, own_main, own_last = gather_rows(units, own_first, obs_site, owner_tile, batch_order, tail)
     oth = lax.ppermute(own, "mem", swap)
     main = lax.ppermute(own_main, "mem", swap)
     last = lax.ppermute(own_last, "mem", swap)
@@ -374,7 +398,7 @@
         rows = rows + lax.ppermute(rows, "tile", [(i, i ^ step) for i in range(n_tile)])
         step *= 2
     mat = chain(rows, obs_value, obs_var, owner_tile, tile_mask, batch_order, tile)
-    out = apply_matrix(mat, ens, first, main, own_last, last)
+    out = apply_matrix(mat, ens.shape, own_first, own_main, own_last, first, main, last)
     return jnp.transpose(out, (1, 0, 2))
 
 

time: 73.1 us -> 69.9 us (0.956)
  starting transfers between devices: 12 us -> 10.2 us
  Pallas kernels: 22.3 us -> 21 us
    ppermute x4, waiting for transfers between devices: 5.87 us -> 8.94 us  [body(): lax.ppermute(rows, 'tile', [(i, i ^ step) for i in range(n_tile)])]
    ppermute x1, waiting for transfers between devices: 32.4 us -> 29.4 us  [body(): oth = lax.ppermute(own, 'mem', swap)]
    ppermute x1, starting transfers between devices: 1.8 us -> 0.29 us  [body(): last = lax.ppermute(own_last, 'mem', swap)]
    ppermute x4, starting transfers between devices: 5.85 us -> 4.96 us  [body(): lax.ppermute(rows, 'tile', [(i, i ^ step) for i in range(n_tile)])]
    pallas_call x2, Pallas kernels: 17.8 us -> 17 us  [the longest x1 14 us: chain(): pl.pallas_call(chain_kernel, out_shape=pltpu.VMEM((2 * half, 2 * members)...]
  transfers between devices with their start and end apart: 8 -> 8, of which waited for: 4 -> 4; matrix products, arithmetic and copies ran while one was open for 0% -> 0% of each run, Pallas kernels for 26% -> 24%
where the time goes in v4:
time: 69.9 us; the launch traced here: 69.7 us
  waiting for transfers between devices  38.3 us (55%)
  Pallas kernels  21 us (30%)
  starting transfers between devices  10.2 us (15%)
    ppermute x1, waiting for transfers between devices, body(): oth = lax.ppermute(own, 'mem', swap)  29.4 us
    pallas_call x1, Pallas kernels, chain(): pl.pallas_call(chain_kernel, out_shape=pltpu.VMEM((2 * half, 2 * members)...  14 us
    ppermute x4, waiting for transfers between devices, body(): lax.ppermute(rows, 'tile', [(i, i ^ step) for i in range(n_tile)])  8.94 us
    ppermute x4, starting transfers between devices, body(): lax.ppermute(rows, 'tile', [(i, i ^ step) for i in range(n_tile)])  4.96 us
    ppermute x1, starting transfers between devices, body(): main = lax.ppermute(own_main, 'mem', swap)  3.06 us
    pallas_call x1, Pallas kernels, apply_matrix(): pl.pallas_call(apply_main, out_shape=state, in_specs=[VMEM] * 4 + [ANY],...  3.02 us
    pallas_call x1, Pallas kernels, gather_rows(): pl.pallas_call(gather_kernel, out_shape=(pltpu.VMEM((2 * half, batches *...  2.07 us
    ppermute x1, starting transfers between devices, body(): first = lax.ppermute(own_first, 'mem', swap)  1.8 us
  transfers between devices with their start and end apart: 8, of which 4 were waited for; matrix products, arithmetic and copies ran while one was open for 0% of the time, Pallas kernels for 24%

profile of v4, /device:TPU:0, one launch (start us, length us, event | category | flops | bytes accessed | tf_op | source)
XLA Modules:
  0.0 69.7 jit_solution(14113388872330251974)
XLA Ops:
  0.0 1.0 %first_units.1.first_ref.own_first_ref = f32[2,16,2048]{2,1,0:T(8,128)S(1)} custom-call(f32[14,16,2048]{2,1,0:T(8,128)} %bitcast.5), custom_call_target="tpu_custom_call" | custom-call | tf_op jit(solution)/shard_map/first_units/pallas_call | solution.py:33
  1.0 0.0 copy-start
  1.0 0.0 copy-start.1
  1.0 0.0 copy-start.2
  1.0 0.0 copy-start.3
  1.0 0.0 copy-start.4
  1.0 2.1 %gather_rows.1 = (f32[32,256]{1,0:T(8,128)S(1)}, f32[10,16,2048]{2,1,0:T(8,128)S(1)}, f32[2,16,2048]{2,1,0:T(8,128)S(1)}) custom-call(s32[8,32]{1,0:T(8,128)} %site_hbm.1, s32[8]{0:T(128)} %owner_ref.1, s32[8]{0:T(128)} %order_ref.1, f32[14,16,2048]{2,1,0:T(8,128)} %bitcast.6, f32[2,16,2048]{2,1,0:T(8,128)S(1)} %first_units.1.first_ref.own_first_ref), custom_call_target="tpu_custom_call" | custom-call | tf_op jit(solution)/shard_map/gather_rows/pallas_call | solution.py:106
  3.1 3.1 %collective-permute-start.7 = (f32[10,16,2048]{2,1,0:T(8,128)S(1)}, f32[10,16,2048]{2,1,0:T(8,128)}, u32[]{:S(2)}, u32[]{:S(2)}) collective-permute-start(f32[10,16,2048]{2,1,0:T(8,128)S(1)} %get-tuple-element.10.own_main_ref), channel_id=1, source_target_pairs={{0,1},{1,0},{2,3},{3,2},{4,5},{5,4},{6,7},{7,6},{8,9},{9,8},{10,11... | collective-permute-start | bytes 3932168 | tf_op jit(solution)/shard_map/ppermute | solution.py:393
  6.2 0.1 collective-permute-start
  6.2 29.4 %collective-permute-done = f32[32,256]{1,0:T(8,128)S(1)} collective-permute-done((f32[32,256]{1,0:T(8,128)S(1)}, f32[32,256]{1,0:T(8,128)S(1)}, u32[]{:S(2)}, u32[]{:S(2)}) %collective-permute-start) | collective-permute-done | bytes 32800 | tf_op jit(solution)/shard_map/ppermute | solution.py:392
  35.6 0.0 collective-permute-start.1
  35.6 1.8 %collective-permute-start.6 = (f32[2,16,2048]{2,1,0:T(8,128)S(1)}, f32[2,16,2048]{2,1,0:T(8,128)S(1)}, u32[]{:S(2)}, u32[]{:S(2)}) collective-permute-start(f32[2,16,2048]{2,1,0:T(8,128)S(1)} %first_units.1.first_ref.own_first_ref), channel_id=1, source_target_pairs={{0,1},{1,0},{2,3},{3,2},{4,5},{5,4},{6,7},{7,6},{8,9},{9,8},{10,11... | collective-permute-start | bytes 786440 | tf_op jit(solution)/shard_map/ppermute | solution.py:390
  37.4 0.3 collective-permute-start.5
  37.7 0.0 collective-permute-done.1
  37.8 1.1 %collective-permute-start.2 = (f32[64,256]{1,0:T(8,128)S(1)}, f32[64,256]{1,0:T(8,128)S(1)}, u32[]{:S(2)}, u32[]{:S(2)}) collective-permute-start(f32[64,256]{1,0:T(8,128)S(1)} %add.12), channel_id=1, source_target_pairs={{0,4},{2,6},{4,0},{6,2},{8,12},{10,14},{12,8},{14,10},{16,20},{18,... | collective-permute-start | bytes 196616 | tf_op jit(solution)/shard_map/ppermute | solution.py:398
  38.9 3.2 %collective-permute-done.2 = f32[64,256]{1,0:T(8,128)S(1)} collective-permute-done((f32[64,256]{1,0:T(8,128)S(1)}, f32[64,256]{1,0:T(8,128)S(1)}, u32[]{:S(2)}, u32[]{:S(2)}) %collective-permute-start.2) | collective-permute-done | bytes 65568 | tf_op jit(solution)/shard_map/ppermute | solution.py:398
  42.1 1.4 %collective-permute-start.3 = (f32[64,256]{1,0:T(8,128)S(1)}, f32[64,256]{1,0:T(8,128)S(1)}, u32[]{:S(2)}, u32[]{:S(2)}) collective-permute-start(f32[64,256]{1,0:T(8,128)S(1)} %add.13), channel_id=1, source_target_pairs={{0,8},{2,10},{4,12},{6,14},{8,0},{10,2},{12,4},{14,6},{16,24},{18,... | collective-permute-start | bytes 196616 | tf_op jit(solution)/shard_map/ppermute | solution.py:398
  43.5 3.0 %collective-permute-done.3 = f32[64,256]{1,0:T(8,128)S(1)} collective-permute-done((f32[64,256]{1,0:T(8,128)S(1)}, f32[64,256]{1,0:T(8,128)S(1)}, u32[]{:S(2)}, u32[]{:S(2)}) %collective-permute-start.3) | collective-permute-done | bytes 65568 | tf_op jit(solution)/shard_map/ppermute | solution.py:398
  46.4 2.5 %collective-permute-start.4 = (f32[64,256]{1,0:T(8,128)S(1)}, f32[64,256]{1,0:T(8,128)S(1)}, u32[]{:S(2)}, u32[]{:S(2)}) collective-permute-start(f32[64,256]{1,0:T(8,128)S(1)} %add.14), channel_id=1, source_target_pairs={{0,16},{2,18},{4,20},{6,22},{8,24},{10,26},{12,28},{14,30},{16,0},... | collective-permute-start | bytes 196616 | tf_op jit(solution)/shard_map/ppermute | solution.py:398
  48.9 2.8 %collective-permute-done.4 = f32[64,256]{1,0:T(8,128)S(1)} collective-permute-done((f32[64,256]{1,0:T(8,128)S(1)}, f32[64,256]{1,0:T(8,128)S(1)}, u32[]{:S(2)}, u32[]{:S(2)}) %collective-permute-start.4) | collective-permute-done | bytes 65568 | tf_op jit(solution)/shard_map/ppermute | solution.py:398
  51.7 0.0 copy-done
  51.7 0.0 copy-done.1
  51.7 0.0 copy-done.2
  51.7 0.0 copy-done.3
  51.7 0.0 copy-done.4
  51.7 14.0 %chain.1.mat_ref = bf16[64,128]{1,0:T(8,128)(2,1)S(1)} custom-call(s32[8]{0:T(128)S(1)} %copy-done.3, s32[8]{0:T(128)S(1)} %copy-done.4, s32[8,16]{1,0:T(8,128)S(1)} %copy-done, f32[8,32]{1,0:T(8,128)S(1)} %copy-done.1, s32[1]{0:T(128)} %bitcast.tile_ref, f32[64,256]{1,0:T(8,128)S(1)} %add.15.raw_ref, f32[8,32]{1,0:T(8,128)S(1)} %copy-done.2), custom_call_target="tpu_custom_call" | custom-call | tf_op jit(solution)/shard_map/chain/pallas_call | solution.py:282
  65.7 0.0 collective-permute-done.6.first_ref
  65.7 0.0 collective-permute-done.7.main_hbm
  65.8 3.0 %apply_main.1.prev_hbm = f32[7,32,2048]{2,1,0:T(8,128)} custom-call(bf16[64,128]{1,0:T(8,128)(2,1)S(1)} %chain.1.mat_ref, f32[2,16,2048]{2,1,0:T(8,128)S(1)} %first_units.1.first_ref.own_first_ref, f32[10,16,2048]{2,1,0:T(8,128)S(1)} %get-tuple-element.10.own_main_ref, f32[2,16,2048]{2,1,0:T(8,128)S(1)} %collective-permute-done.6.first_ref, ...), custom_call_target="tpu_custom_call" | custom-call | tf_op jit(solution)/shard_map/apply_main/pallas_call | solution.py:355
  68.8 0.0 collective-permute-done.5.last_ref
  68.8 0.9 %apply_last.1 = f32[7,32,2048]{2,1,0:T(8,128)} custom-call(bf16[64,128]{1,0:T(8,128)(2,1)S(1)} %chain.1.mat_ref, f32[2,16,2048]{2,1,0:T(8,128)S(1)} %get-tuple-element.9.own_ref, f32[2,16,2048]{2,1,0:T(8,128)S(1)} %collective-permute-done.5.last_ref, f32[7,32,2048]{2,1,0:T(8,128)} %apply_main.1.prev_hbm), custom_call_target="tpu_custom_call", output_to_operand_aliasing={{}: (3, {})} | custom-call | tf_op jit(solution)/shard_map/apply_last/pallas_call | solution.py:369
  (6 shorter events, 0.0 us)
Async XLA Ops:
  1.0 50.7 %copy-start = (s32[8,16]{1,0:T(8,128)S(1)}, s32[8,16]{1,0:T(8,128)}, u32[]{:S(2)}) copy-start(s32[8,16]{1,0:T(8,128)} %mask_ref.1) | copy-start | bytes 1540
  1.0 50.7 %copy-start.1 = (f32[8,32]{1,0:T(8,128)S(1)}, f32[8,32]{1,0:T(8,128)}, u32[]{:S(2)}) copy-start(f32[8,32]{1,0:T(8,128)} %var_ref.1) | copy-start | bytes 3076
  1.0 50.7 %copy-start.2 = (f32[8,32]{1,0:T(8,128)S(1)}, f32[8,32]{1,0:T(8,128)}, u32[]{:S(2)}) copy-start(f32[8,32]{1,0:T(8,128)} %val_ref.1) | copy-start | bytes 3076
  1.0 50.7 %copy-start.3 = (s32[8]{0:T(128)S(1)}, s32[8]{0:T(128)}, u32[]{:S(2)}) copy-start(s32[8]{0:T(128)} %order_ref.1) | copy-start | bytes 100
  1.0 50.7 %copy-start.4 = (s32[8]{0:T(128)S(1)}, s32[8]{0:T(128)}, u32[]{:S(2)}) copy-start(s32[8]{0:T(128)} %owner_ref.1) | copy-start | bytes 100
  3.1 62.6 %collective-permute-start.7 = (f32[10,16,2048]{2,1,0:T(8,128)S(1)}, f32[10,16,2048]{2,1,0:T(8,128)}, u32[]{:S(2)}, u32[]{:S(2)}) collective-permute-start(f32[10,16,2048]{2,1,0:T(8,128)S(1)} %get-tuple-element.10.own_main_ref), channel_id=1, source_target_pairs={{0,1},{1,0},{2,3},{3,2},{4,5},{5,4},{6,7},{7,6},{8,9},{9,8},{10,11... | collective-permute-start | bytes 3932168 | tf_op jit(solution)/shard_map/ppermute | solution.py:393
  6.2 29.5 %collective-permute-start = (f32[32,256]{1,0:T(8,128)S(1)}, f32[32,256]{1,0:T(8,128)S(1)}, u32[]{:S(2)}, u32[]{:S(2)}) collective-permute-start(f32[32,256]{1,0:T(8,128)S(1)} %get-tuple-element.8), channel_id=1, source_target_pairs={{0,1},{1,0},{2,3},{3,2},{4,5},{5,4},{6,7},{7,6},{8,9},{9,8},{10,11... | collective-permute-start | bytes 98312 | tf_op jit(solution)/shard_map/ppermute | solution.py:392
  35.6 2.1 %collective-permute-start.1 = (f32[64,256]{1,0:T(8,128)S(1)}, f32[64,256]{1,0:T(8,128)S(1)}, u32[]{:S(2)}, u32[]{:S(2)}) collective-permute-start(f32[64,256]{1,0:T(8,128)S(1)} %constant_dynamic-update-slice_fusion), channel_id=1, source_target_pairs={{0,2},{2,0},{4,6},{6,4},{8,10},{10,8},{12,14},{14,12},{16,18},{18,... | collective-permute-start | bytes 196616 | tf_op jit(solution)/shard_map/ppermute | solution.py:398
  35.6 30.1 %collective-permute-start.6 = (f32[2,16,2048]{2,1,0:T(8,128)S(1)}, f32[2,16,2048]{2,1,0:T(8,128)S(1)}, u32[]{:S(2)}, u32[]{:S(2)}) collective-permute-start(f32[2,16,2048]{2,1,0:T(8,128)S(1)} %first_units.1.first_ref.own_first_ref), channel_id=1, source_target_pairs={{0,1},{1,0},{2,3},{3,2},{4,5},{5,4},{6,7},{7,6},{8,9},{9,8},{10,11... | collective-permute-start | bytes 786440 | tf_op jit(solution)/shard_map/ppermute | solution.py:390
  37.4 31.3 %collective-permute-start.5 = (f32[2,16,2048]{2,1,0:T(8,128)S(1)}, f32[2,16,2048]{2,1,0:T(8,128)S(1)}, u32[]{:S(2)}, u32[]{:S(2)}) collective-permute-start(f32[2,16,2048]{2,1,0:T(8,128)S(1)} %get-tuple-element.9.own_ref), channel_id=1, source_target_pairs={{0,1},{1,0},{2,3},{3,2},{4,5},{5,4},{6,7},{7,6},{8,9},{9,8},{10,11... | collective-permute-start | bytes 786440 | tf_op jit(solution)/shard_map/ppermute | solution.py:394
  37.8 4.3 %collective-permute-start.2 = (f32[64,256]{1,0:T(8,128)S(1)}, f32[64,256]{1,0:T(8,128)S(1)}, u32[]{:S(2)}, u32[]{:S(2)}) collective-permute-start(f32[64,256]{1,0:T(8,128)S(1)} %add.12), channel_id=1, source_target_pairs={{0,4},{2,6},{4,0},{6,2},{8,12},{10,14},{12,8},{14,10},{16,20},{18,... | collective-permute-start | bytes 196616 | tf_op jit(solution)/shard_map/ppermute | solution.py:398
  42.1 4.3 %collective-permute-start.3 = (f32[64,256]{1,0:T(8,128)S(1)}, f32[64,256]{1,0:T(8,128)S(1)}, u32[]{:S(2)}, u32[]{:S(2)}) collective-permute-start(f32[64,256]{1,0:T(8,128)S(1)} %add.13), channel_id=1, source_target_pairs={{0,8},{2,10},{4,12},{6,14},{8,0},{10,2},{12,4},{14,6},{16,24},{18,... | collective-permute-start | bytes 196616 | tf_op jit(solution)/shard_map/ppermute | solution.py:398
  46.4 5.2 %collective-permute-start.4 = (f32[64,256]{1,0:T(8,128)S(1)}, f32[64,256]{1,0:T(8,128)S(1)}, u32[]{:S(2)}, u32[]{:S(2)}) collective-permute-start(f32[64,256]{1,0:T(8,128)S(1)} %add.14), channel_id=1, source_target_pairs={{0,16},{2,18},{4,20},{6,22},{8,24},{10,26},{12,28},{14,30},{16,0},... | collective-permute-start | bytes 196616 | tf_op jit(solution)/shard_map/ppermute | solution.py:398

commit v5 on v4

--- a/solution.py
+++ b/solution.py
@@ -134,10 +134,10 @@
         [jnp.concatenate([high, high], axis=1), jnp.concatenate([low, jnp.zeros_like(low)], axis=1)], axis=0)
 
 
-def chain_kernel(order_ref, owner_ref, mask_ref, var_ref, tile_ref, raw_ref, val_ref,
-                 out_ref, w_ref, left_ref, right_ref, z_ref, v_ref, val_s):
+def chain_kernel(order_ref, owner_ref, mask_ref, var_ref, tile_ref, part_ref, back_ref, val_ref,
+                 out_ref, w_ref, left_ref, right_ref, z_ref, v_ref, val_s, cov_ref):
     batches, obs = val_ref.shape
-    members = raw_ref.shape[0]
+    members = part_ref.shape[0]
     half = members // 2
     total = batches * obs
     tiles = total // LANES
@@ -165,7 +165,9 @@
         values.append(row)
     values = jnp.concatenate(values, axis=1)
 
-    raw = raw_ref[...]
+    part, back = part_ref[...], back_ref[...]
+    even = lax.rem(tile, 2) == 0
+    raw = jnp.concatenate([jnp.where(even, part, back), jnp.where(even, back, part)], axis=1)
     mean = jnp.sum(raw, axis=0, keepdims=True) * (1.0 / members)
     anom = raw - mean
     first = lax.broadcasted_iota(jnp.int32, (SUBS, total), 0) == 0
@@ -213,51 +215,58 @@
         gram = pltpu.roll(gram, shift, 1)
         cols = [[jnp.broadcast_to(gram[i * SUBS:(i + 1) * SUBS, j:j + 1], (SUBS, LANES)) if i >= j // SUBS else None
                  for i in range(blocks)] for j in range(obs)]
-        for k in range(0, obs, 2):
-            kb, ks = k // SUBS, k % SUBS
-            one, two = cols[k], cols[k + 1]
-            var1, var2 = var_ref[b, k], var_ref[b, k + 1]
-            cross = spread(one[kb][ks + 1:ks + 2, :])
-            total1 = spread(one[kb][ks:ks + 1, :]) + var1
-            total2 = spread(two[kb][ks + 1:ks + 2, :]) + var2
-            g1 = 1.0 / total1
-            g2 = total1 * (1.0 / (total1 * total2 - cross * cross))
-            ratio = g1 * cross
-            for j in range(k + 2, obs):
-                jb, js = j // SUBS, j % SUBS
-                h1 = spread(one[jb][js:js + 1, :])
-                h2 = spread(two[jb][js:js + 1, :])
-                f2 = g2 * (h2 - ratio * h1)
-                f1 = g1 * h1 - ratio * f2
-                for i in range(jb, blocks):
-                    cols[j][i] = cols[j][i] - (one[i] * f1 + two[i] * f2)
-            moved = [two[i] - one[i] * ratio if two[i] is not None else None for i in range(blocks)]
-            below1 = [None] * kb + [jnp.where(sub8 > ks, one[kb], 0.0)] + one[kb + 1:]
-            below2 = [None] * kb + [jnp.where(sub8 > ks + 1, moved[kb], 0.0)] + moved[kb + 1:]
-            beta1 = g1 / (1.0 + jnp.sqrt(var1 * g1))
-            beta2 = g2 / (1.0 + jnp.sqrt(var2 * g2))
+        gains, alphas = [], []
+        for e in range(blocks):
+            gain8 = jnp.zeros((SUBS, LANES), jnp.float32)
+            ratio8 = jnp.zeros((SUBS, LANES), jnp.float32)
+            scaled = []
+            for r in range(SUBS):
+                k = e * SUBS + r
+                col = cols[k]
+                var = var_ref[b, k]
+                g = 1.0 / (spread(col[e][r:r + 1, :]) + var)
+                gain8 = jnp.where(sub8 == r, g, gain8)
+                ratio8 = jnp.where(sub8 == r, var * g, ratio8)
+                scale = [None] * e + [col[i] * g for i in range(e, blocks)]
+                for i in range(e, blocks):
+                    cov_ref[k, i * SUBS:(i + 1) * SUBS, :] = col[i]
+                for n in range(k + 1, obs):
+                    if n == k + 1:
+                        factor = spread(col[n // SUBS][n % SUBS:n % SUBS + 1, :])
+                    else:
+                        factor = cov_ref[k, pl.ds(n, SUBS, stride=0), :]
+                    for i in range(n // SUBS, blocks):
+                        cols[n][i] = cols[n][i] - scale[i] * factor
+                scale[e] = jnp.where(sub8 > r, scale[e], 0.0)
+                scaled.append(scale)
+            alpha8 = 1.0 / (1.0 + jnp.sqrt(ratio8))
+            gains.append(gain8)
+            alphas.append(alpha8)
+            for r in range(SUBS):
+                alpha = spread(alpha8[r:r + 1, :])
+                for t in range(width):
+                    u = spread(wp[t][e][r:r + 1, :])
+                    both = jnp.where(pick_w[t], u, alpha * u)
+                    for i in range(e, blocks):
+                        wp[t][i] = wp[t][i] - scaled[r][i] * both
+        for i in range(blocks):
+            gain = gains[i] * inv
+            alpha = alphas[i]
+            own = slice(i * SUBS, (i + 1) * SUBS)
+            off = slice(obs + i * SUBS, obs + (i + 1) * SUBS)
             for t in range(width):
-                u1 = spread(wp[t][kb][ks:ks + 1, :])
-                both1 = jnp.where(pick_w[t], g1, beta1) * u1
-                u2 = spread(wp[t][kb][ks + 1:ks + 2, :]) - cross * both1
-                both2 = jnp.where(pick_w[t], g2, beta2) * u2
                 here = slice(t * LANES, (t + 1) * LANES)
-                right_ref[k:k + 1, here] = both1[:1]
-                right_ref[k + 1:k + 2, here] = both2[:1]
-                right_ref[obs + k:obs + k + 1, here] = (jnp.where(pick_b[t], beta1, 0.0) * u1)[:1]
-                right_ref[obs + k + 1:obs + k + 2, here] = (jnp.where(pick_b[t], beta2, 0.0) * u2)[:1]
-                for i in range(kb, blocks):
-                    wp[t][i] = wp[t][i] - (below1[i] * both1 + below2[i] * both2)
-        for t in range(tiles):
-            for i in range(blocks):
-                d = wp[t][i] * (late[t] * inv)
-                left_ref[i * SUBS:(i + 1) * SUBS, t * LANES:(t + 1) * LANES] = d * act[t]
-                left_ref[obs + i * SUBS:obs + (i + 1) * SUBS, t * LANES:(t + 1) * LANES] = d * (1.0 - act[t])
-        for i in range(blocks):
+                reduced = alpha * wp[t][i]
+                right_ref[own, here] = jnp.where(pick_w[t], wp[t][i], reduced)
+                right_ref[off, here] = jnp.where(pick_b[t], reduced, 0.0)
+                if t < tiles:
+                    d = wp[t][i] * (late[t] * gain)
+                    left_ref[own, here] = d * act[t]
+                    left_ref[off, here] = d * (1.0 - act[t])
             at = pl.ds(pl.multiple_of(start + i * SUBS, SUBS), SUBS)
             z_ref[at, :] = wp[tiles][i] * mine_f
-        gain = jnp.broadcast_to(right_ref[:obs, (width - 1) * LANES:(width - 1) * LANES + 1], (obs, LANES))
-        v_ref[rows, :] = (gain - right_ref[:obs, tiles * LANES:(tiles + 1) * LANES]) * inv
+            miss = jnp.broadcast_to(wp[width - 1][i][:, :1], (SUBS, LANES))
+            v_ref[at, :] = (miss - alpha * wp[tiles][i]) * gain
 
         for low in range(tiles):
             @pl.when((p < batches - 1) & (lax.div(p + 1, per) == low))
@@ -273,8 +282,8 @@
     out_ref[...] = left_factor(moved[members:members + half, :members])
 
 
-def chain(rows, obs_value, obs_var, owner_tile, tile_mask, batch_order, tile):
-    members, total = rows.shape
+def chain(part, back, obs_value, obs_var, owner_tile, tile_mask, batch_order, tile):
+    members, total = part.shape[0], 2 * part.shape[1]
     half = members // 2
     obs = obs_value.shape[1]
     width = total // LANES + 2
@@ -282,7 +291,7 @@
     return pl.pallas_call(
         chain_kernel,
         out_shape=pltpu.VMEM((2 * half, 2 * members), jnp.bfloat16),
-        in_specs=[SMEM] * 5 + [VMEM] * 2,
+        in_specs=[SMEM] * 5 + [VMEM] * 3,
         out_specs=VMEM,
         scratch_shapes=[
             pltpu.VMEM((width, total, LANES), f32),
@@ -291,10 +300,11 @@
             pltpu.VMEM((total, LANES), f32),
             pltpu.VMEM((total, LANES), f32),
             pltpu.VMEM((obs_value.shape[0], LANES), f32),
+            pltpu.VMEM((obs, obs, LANES), f32),
         ],
         compiler_params=pltpu.CompilerParams(vmem_limit_bytes=8 << 20),
         name="chain",
-    )(batch_order, owner_tile, tile_mask, obs_var, tile, vmem(rows), obs_value)
+    )(batch_order, owner_tile, tile_mask, obs_var, tile, vmem(part), vmem(back), obs_value)
 
 
 def apply_block(left, own, upper, lower):
@@ -306,17 +316,10 @@
     return own + (y[:half] + y[half:])
 
 
-def apply_main(mat_ref, own_first_ref, own_main_ref, first_ref, main_hbm, out_hbm, main_ref, new_ref, sem_in, sem_out):
+def apply_main(mat_ref, own_first_ref, own_main_ref, first_ref, main_ref, out_hbm, new_ref, sem_out):
     chans = new_ref.shape[0]
     ahead = first_ref.shape[0]
     stores = [pltpu.make_async_copy(new_ref.at[c], out_hbm.at[c], sem_out.at[c]) for c in range(chans)]
-    loads = []
-    for c in range(chans):
-        low, high = max(2 * c - ahead, 0), max(2 * c + 2 - ahead, 0)
-        part = pl.ds(low, high - low)
-        loads.append(pltpu.make_async_copy(main_hbm.at[part], main_ref.at[part], sem_in.at[c]) if high > low else None)
-        if high > low:
-            loads[c].start()
     left = mat_ref[...]
 
     def pair(a, b, c):
@@ -324,8 +327,6 @@
 
     for c in range(chans):
         own = jnp.concatenate(pair(own_first_ref, own_main_ref, c), axis=0)
-        if loads[c] is not None:
-            loads[c].wait()
         new_ref[c] = apply_block(left, own, *pair(first_ref, main_ref, c))
         stores[c].start()
     for store in stores:
@@ -355,17 +356,12 @@
     out = pl.pallas_call(
         apply_main,
         out_shape=state,
-        in_specs=[VMEM] * 4 + [ANY],
+        in_specs=[VMEM] * 5,
         out_specs=ANY,
-        scratch_shapes=[
-            pltpu.VMEM(main.shape, f32),
-            pltpu.VMEM((head, half, cells), f32),
-            pltpu.SemaphoreType.DMA((head,)),
-            pltpu.SemaphoreType.DMA((head,)),
-        ],
+        scratch_shapes=[pltpu.VMEM((head, half, cells), f32), pltpu.SemaphoreType.DMA((head,))],
         compiler_params=params,
         name="apply_main",
-    )(vmem(mat), vmem(own_first), vmem(own_main), vmem(first), hbm(main))
+    )(vmem(mat), vmem(own_first), vmem(own_main), vmem(first), vmem(main))
     return pl.pallas_call(
         apply_last,
         out_shape=state,
@@ -385,19 +381,27 @@
     ens = jnp.transpose(ensemble, (1, 0, 2))
     chans, half, cells = ens.shape
     units = ens.reshape(2 * chans, half // 2, cells)
-    head, tail = 2, 2
+    head, tail = 3, 2
+
+    def across(x, step):
+        return lax.ppermute(x, "tile", [(i, i ^ step) for i in range(n_tile)])
+
     own_first = first_units(units, head)
     first = lax.ppermute(own_first, "mem", swap)
     own, own_main, own_last = gather_rows(units, own_first, obs_site, owner_tile, batch_order, tail)
+    own = own + across(own, 1)
+    cut = own.shape[1] // 2
+    own = jnp.where(lax.rem(tile[0], 2) == 0, own[:, :cut], own[:, cut:])
     oth = lax.ppermute(own, "mem", swap)
     main = lax.ppermute(own_main, "mem", swap)
     last = lax.ppermute(own_last, "mem", swap)
-    rows = jnp.concatenate([own, oth], axis=0)
-    step = 1
+    part = jnp.concatenate([own, oth], axis=0)
+    step = 2
     while step < n_tile:
-        rows = rows + lax.ppermute(rows, "tile", [(i, i ^ step) for i in range(n_tile)])
+        part = part + across(part, step)
         step *= 2
-    mat = chain(rows, obs_value, obs_var, owner_tile, tile_mask, batch_order, tile)
+    back = lax.ppermute(part, "tile", [(i, i ^ 1) for i in range(n_tile)])
+    mat = chain(part, back, obs_value, obs_var, owner_tile, tile_mask, batch_order, tile)
     out = apply_matrix(mat, ens.shape, own_first, own_main, own_last, first, main, last)
     return jnp.transpose(out, (1, 0, 2))
 

time: 69.9 us -> 61.3 us (0.88)
  waiting for transfers between devices: 38.3 us -> 31.7 us
  Pallas kernels: 21 us -> 16.9 us
  starting transfers between devices: 10.2 us -> 12.4 us
    ppermute x1, waiting for transfers between devices: 29.4 us -> 23.9 us  [body(): oth = lax.ppermute(own, 'mem', swap)]
    pallas_call x1, Pallas kernels: 14 us -> 11.4 us  [chain(): pl.pallas_call(chain_kernel, out_shape=pltpu.VMEM((2 * half, 2 * members)...]
    pallas_call x1, Pallas kernels: 3.02 us -> 1.42 us  [apply_matrix(): pl.pallas_call(apply_main, out_shape=state, in_specs=[VMEM] * 5, out_spec...]
    ppermute x1, starting transfers between devices: 0.29 us -> 1.52 us  [body(): last = lax.ppermute(own_last, 'mem', swap)]
    ppermute x4 -> x5, waiting for transfers between devices: 8.94 us -> 7.86 us  [the longest x4 6.67 us: across(): return lax.ppermute(x, 'tile', [(i, i ^ step) for i in range(n_tile)])]
    ppermute x4 -> x5, starting transfers between devices: 4.96 us -> 5.72 us  [the longest x4 5.72 us: across(): return lax.ppermute(x, 'tile', [(i, i ^ step) for i in range(n_tile)])]
  transfers between devices with their start and end apart: 8 -> 9, of which waited for: 4 -> 6; matrix products, arithmetic and copies ran while one was open for 0% -> 0% of each run, Pallas kernels for 24% -> 21%
where the time goes in v5:
time: 61.3 us; the launch traced here: 61.2 us
  waiting for transfers between devices  31.7 us (52%)
  Pallas kernels  16.9 us (28%)
  starting transfers between devices  12.4 us (20%)
    ppermute x1, waiting for transfers between devices, body(): oth = lax.ppermute(own, 'mem', swap)  23.9 us
    pallas_call x1, Pallas kernels, chain(): pl.pallas_call(chain_kernel, out_shape=pltpu.VMEM((2 * half, 2 * members)...  11.4 us
    ppermute x4, waiting for transfers between devices, across(): return lax.ppermute(x, 'tile', [(i, i ^ step) for i in range(n_tile)])  6.67 us
    ppermute x4, starting transfers between devices, across(): return lax.ppermute(x, 'tile', [(i, i ^ step) for i in range(n_tile)])  5.72 us
    ppermute x1, starting transfers between devices, body(): main = lax.ppermute(own_main, 'mem', swap)  3.06 us
    pallas_call x1, Pallas kernels, gather_rows(): pl.pallas_call(gather_kernel, out_shape=(pltpu.VMEM((2 * half, batches *...  2.06 us
    ppermute x1, starting transfers between devices, body(): first = lax.ppermute(own_first, 'mem', swap)  1.95 us
    ppermute x1, starting transfers between devices, body(): last = lax.ppermute(own_last, 'mem', swap)  1.52 us
  transfers between devices with their start and end apart: 9, of which 6 were waited for; matrix products, arithmetic and copies ran while one was open for 0% of the time, Pallas kernels for 21%

profile of v5, /device:TPU:0, one launch (start us, length us, event | category | flops | bytes accessed | tf_op | source)
XLA Modules:
  0.0 61.2 jit_solution(2411244400236905116)
XLA Ops:
  0.0 1.0 %first_units.1.first_ref.own_first_ref = f32[3,16,2048]{2,1,0:T(8,128)S(1)} custom-call(f32[14,16,2048]{2,1,0:T(8,128)} %bitcast.5), custom_call_target="tpu_custom_call" | custom-call | tf_op jit(solution)/shard_map/first_units/pallas_call | solution.py:33
  1.0 0.0 copy-start
  1.0 0.0 copy-start.1
  1.0 0.0 copy-start.2
  1.0 0.0 copy-start.3
  1.1 0.0 copy-start.4
  1.1 2.1 %gather_rows.1 = (f32[32,256]{1,0:T(8,128)S(1)}, f32[9,16,2048]{2,1,0:T(8,128)S(1)}, f32[2,16,2048]{2,1,0:T(8,128)S(1)}) custom-call(s32[8,32]{1,0:T(8,128)} %site_hbm.1, s32[8]{0:T(128)} %owner_ref.1, s32[8]{0:T(128)} %order_ref.1, f32[14,16,2048]{2,1,0:T(8,128)} %bitcast.6, f32[3,16,2048]{2,1,0:T(8,128)S(1)} %first_units.1.first_ref.own_first_ref), custom_call_target="tpu_custom_call" | custom-call | tf_op jit(solution)/shard_map/gather_rows/pallas_call | solution.py:106
  3.1 3.1 %collective-permute-start.8 = (f32[9,16,2048]{2,1,0:T(8,128)S(1)}, f32[9,16,2048]{2,1,0:T(8,128)S(1)}, u32[]{:S(2)}, u32[]{:S(2)}) collective-permute-start(f32[9,16,2048]{2,1,0:T(8,128)S(1)} %get-tuple-element.10.own_main_ref), channel_id=1, source_target_pairs={{0,1},{1,0},{2,3},{3,2},{4,5},{5,4},{6,7},{7,6},{8,9},{9,8},{10,11... | collective-permute-start | bytes 3538952 | tf_op jit(solution)/shard_map/ppermute | solution.py:396
  6.2 0.0 collective-permute-start
  6.2 1.2 %collective-permute-done = f32[32,256]{1,0:T(8,128)S(1)} collective-permute-done((f32[32,256]{1,0:T(8,128)S(1)}, f32[32,256]{1,0:T(8,128)S(1)}, u32[]{:S(2)}, u32[]{:S(2)}) %collective-permute-start) | collective-permute-done | bytes 32800 | tf_op jit(solution)/shard_map/ppermute | solution.py:387
  7.4 0.1 collective-permute-start.1
  7.6 1.9 %collective-permute-start.7 = (f32[3,16,2048]{2,1,0:T(8,128)S(1)}, f32[3,16,2048]{2,1,0:T(8,128)S(1)}, u32[]{:S(2)}, u32[]{:S(2)}) collective-permute-start(f32[3,16,2048]{2,1,0:T(8,128)S(1)} %first_units.1.first_ref.own_first_ref), channel_id=1, source_target_pairs={{0,1},{1,0},{2,3},{3,2},{4,5},{5,4},{6,7},{7,6},{8,9},{9,8},{10,11... | collective-permute-start | bytes 1179656 | tf_op jit(solution)/shard_map/ppermute | solution.py:390
  9.5 23.9 %collective-permute-done.1 = f32[32,128]{1,0:T(8,128)S(1)} collective-permute-done((f32[32,128]{1,0:T(8,128)S(1)}, f32[32,128]{1,0:T(8,128)S(1)}, u32[]{:S(2)}, u32[]{:S(2)}) %collective-permute-start.1) | collective-permute-done | bytes 16416 | tf_op jit(solution)/shard_map/ppermute | solution.py:395
  33.4 1.3 %collective-permute-start.2 = (f32[64,128]{1,0:T(8,128)S(1)}, f32[64,128]{1,0:T(8,128)S(1)}, u32[]{:S(2)}, u32[]{:S(2)}) collective-permute-start(f32[64,128]{1,0:T(8,128)S(1)} %pad_maximum_fusion), channel_id=1, source_target_pairs={{0,4},{2,6},{4,0},{6,2},{8,12},{10,14},{12,8},{14,10},{16,20},{18,... | collective-permute-start | bytes 98312 | tf_op jit(solution)/shard_map/ppermute | solution.py:387
  34.7 1.5 %collective-permute-start.6 = (f32[2,16,2048]{2,1,0:T(8,128)S(1)}, f32[2,16,2048]{2,1,0:T(8,128)S(1)}, u32[]{:S(2)}, u32[]{:S(2)}) collective-permute-start(f32[2,16,2048]{2,1,0:T(8,128)S(1)} %get-tuple-element.9.own_ref), channel_id=1, source_target_pairs={{0,1},{1,0},{2,3},{3,2},{4,5},{5,4},{6,7},{7,6},{8,9},{9,8},{10,11... | collective-permute-start | bytes 786440 | tf_op jit(solution)/shard_map/ppermute | solution.py:397
  36.2 1.1 %collective-permute-done.2 = f32[64,128]{1,0:T(8,128)S(1)} collective-permute-done((f32[64,128]{1,0:T(8,128)S(1)}, f32[64,128]{1,0:T(8,128)S(1)}, u32[]{:S(2)}, u32[]{:S(2)}) %collective-permute-start.2) | collective-permute-done | bytes 32800 | tf_op jit(solution)/shard_map/ppermute | solution.py:387
  37.3 2.1 %collective-permute-start.3 = (f32[64,128]{1,0:T(8,128)S(1)}, f32[64,128]{1,0:T(8,128)S(1)}, u32[]{:S(2)}, u32[]{:S(2)}) collective-permute-start(f32[64,128]{1,0:T(8,128)S(1)} %fusion), channel_id=1, source_target_pairs={{0,8},{2,10},{4,12},{6,14},{8,0},{10,2},{12,4},{14,6},{16,24},{18,... | collective-permute-start | bytes 98312 | tf_op jit(solution)/shard_map/ppermute | solution.py:387
  39.4 1.9 %collective-permute-done.3 = f32[64,128]{1,0:T(8,128)S(1)} collective-permute-done((f32[64,128]{1,0:T(8,128)S(1)}, f32[64,128]{1,0:T(8,128)S(1)}, u32[]{:S(2)}, u32[]{:S(2)}) %collective-permute-start.3) | collective-permute-done | bytes 32800 | tf_op jit(solution)/shard_map/ppermute | solution.py:387
  41.3 2.3 %collective-permute-start.4 = (f32[64,128]{1,0:T(8,128)S(1)}, f32[64,128]{1,0:T(8,128)S(1)}, u32[]{:S(2)}, u32[]{:S(2)}) collective-permute-start(f32[64,128]{1,0:T(8,128)S(1)} %add.14), channel_id=1, source_target_pairs={{0,16},{2,18},{4,20},{6,22},{8,24},{10,26},{12,28},{14,30},{16,0},... | collective-permute-start | bytes 98312 | tf_op jit(solution)/shard_map/ppermute | solution.py:387
  43.6 2.5 %collective-permute-done.4 = f32[64,128]{1,0:T(8,128)S(1)} collective-permute-done((f32[64,128]{1,0:T(8,128)S(1)}, f32[64,128]{1,0:T(8,128)S(1)}, u32[]{:S(2)}, u32[]{:S(2)}) %collective-permute-start.4) | collective-permute-done | bytes 32800 | tf_op jit(solution)/shard_map/ppermute | solution.py:387
  46.1 0.0 collective-permute-start.5
  46.1 1.2 %collective-permute-done.5.back_ref = f32[64,128]{1,0:T(8,128)S(1)} collective-permute-done((f32[64,128]{1,0:T(8,128)S(1)}, f32[64,128]{1,0:T(8,128)S(1)}, u32[]{:S(2)}, u32[]{:S(2)}) %collective-permute-start.5) | collective-permute-done | bytes 32800 | tf_op jit(solution)/shard_map/ppermute | solution.py:403
  47.3 0.0 copy-done
  47.3 0.0 copy-done.1
  47.3 0.0 copy-done.2
  47.3 0.0 copy-done.3
  47.3 0.0 copy-done.4
  47.3 11.4 %chain.1.mat_ref = bf16[64,128]{1,0:T(8,128)(2,1)S(1)} custom-call(s32[8]{0:T(128)S(1)} %copy-done.3, s32[8]{0:T(128)S(1)} %copy-done.4, s32[8,16]{1,0:T(8,128)S(1)} %copy-done, f32[8,32]{1,0:T(8,128)S(1)} %copy-done.1, s32[1]{0:T(128)} %bitcast.tile_ref, f32[64,128]{1,0:T(8,128)S(1)} %add.15.part_ref, f32[64,128]{1,0:T(8,128)S(1)} %collective-permute-done.5.back_ref, ...), custom_call_target="tpu_custom_call" | custom-call | tf_op jit(solution)/shard_map/chain/pallas_call | solution.py:291
  58.8 0.0 collective-permute-done.7.first_ref
  58.8 0.0 collective-permute-done.8.main_ref
  58.8 1.4 %apply_main.1.prev_hbm = f32[7,32,2048]{2,1,0:T(8,128)} custom-call(bf16[64,128]{1,0:T(8,128)(2,1)S(1)} %chain.1.mat_ref, f32[3,16,2048]{2,1,0:T(8,128)S(1)} %first_units.1.first_ref.own_first_ref, f32[9,16,2048]{2,1,0:T(8,128)S(1)} %get-tuple-element.10.own_main_ref, f32[3,16,2048]{2,1,0:T(8,128)S(1)} %collective-permute-done.7.first_ref, ...), custom_call_target="tpu_custom_call" | custom-call | tf_op jit(solution)/shard_map/apply_main/pallas_call | solution.py:356
  60.2 0.0 collective-permute-done.6.last_ref
  60.2 0.9 %apply_last.1 = f32[7,32,2048]{2,1,0:T(8,128)} custom-call(bf16[64,128]{1,0:T(8,128)(2,1)S(1)} %chain.1.mat_ref, f32[2,16,2048]{2,1,0:T(8,128)S(1)} %get-tuple-element.9.own_ref, f32[2,16,2048]{2,1,0:T(8,128)S(1)} %collective-permute-done.6.last_ref, f32[7,32,2048]{2,1,0:T(8,128)} %apply_main.1.prev_hbm), custom_call_target="tpu_custom_call", output_to_operand_aliasing={{}: (3, {})} | custom-call | tf_op jit(solution)/shard_map/apply_last/pallas_call | solution.py:365
  (6 shorter events, 0.0 us)
Async XLA Ops:
  1.0 46.3 %copy-start = (s32[8,16]{1,0:T(8,128)S(1)}, s32[8,16]{1,0:T(8,128)}, u32[]{:S(2)}) copy-start(s32[8,16]{1,0:T(8,128)} %mask_ref.1) | copy-start | bytes 1540
  1.0 46.3 %copy-start.1 = (f32[8,32]{1,0:T(8,128)S(1)}, f32[8,32]{1,0:T(8,128)}, u32[]{:S(2)}) copy-start(f32[8,32]{1,0:T(8,128)} %var_ref.1) | copy-start | bytes 3076
  1.0 46.3 %copy-start.2 = (f32[8,32]{1,0:T(8,128)S(1)}, f32[8,32]{1,0:T(8,128)}, u32[]{:S(2)}) copy-start(f32[8,32]{1,0:T(8,128)} %val_ref.1) | copy-start | bytes 3076
  1.0 46.3 %copy-start.3 = (s32[8]{0:T(128)S(1)}, s32[8]{0:T(128)}, u32[]{:S(2)}) copy-start(s32[8]{0:T(128)} %order_ref.1) | copy-start | bytes 100
  1.1 46.3 %copy-start.4 = (s32[8]{0:T(128)S(1)}, s32[8]{0:T(128)}, u32[]{:S(2)}) copy-start(s32[8]{0:T(128)} %owner_ref.1) | copy-start | bytes 100
  3.1 55.6 %collective-permute-start.8 = (f32[9,16,2048]{2,1,0:T(8,128)S(1)}, f32[9,16,2048]{2,1,0:T(8,128)S(1)}, u32[]{:S(2)}, u32[]{:S(2)}) collective-permute-start(f32[9,16,2048]{2,1,0:T(8,128)S(1)} %get-tuple-element.10.own_main_ref), channel_id=1, source_target_pairs={{0,1},{1,0},{2,3},{3,2},{4,5},{5,4},{6,7},{7,6},{8,9},{9,8},{10,11... | collective-permute-start | bytes 3538952 | tf_op jit(solution)/shard_map/ppermute | solution.py:396
  6.2 1.2 %collective-permute-start = (f32[32,256]{1,0:T(8,128)S(1)}, f32[32,256]{1,0:T(8,128)S(1)}, u32[]{:S(2)}, u32[]{:S(2)}) collective-permute-start(f32[32,256]{1,0:T(8,128)S(1)} %get-tuple-element.8), channel_id=1, source_target_pairs={{0,2},{2,0},{4,6},{6,4},{8,10},{10,8},{12,14},{14,12},{16,18},{18,... | collective-permute-start | bytes 98312 | tf_op jit(solution)/shard_map/ppermute | solution.py:387
  7.4 25.9 %collective-permute-start.1 = (f32[32,128]{1,0:T(8,128)S(1)}, f32[32,128]{1,0:T(8,128)S(1)}, u32[]{:S(2)}, u32[]{:S(2)}) collective-permute-start(f32[32,128]{1,0:T(8,128)S(1)} %slice_select_fusion), channel_id=1, source_target_pairs={{0,1},{1,0},{2,3},{3,2},{4,5},{5,4},{6,7},{7,6},{8,9},{9,8},{10,11... | collective-permute-start | bytes 49160 | tf_op jit(solution)/shard_map/ppermute | solution.py:395
  7.6 51.2 %collective-permute-start.7 = (f32[3,16,2048]{2,1,0:T(8,128)S(1)}, f32[3,16,2048]{2,1,0:T(8,128)S(1)}, u32[]{:S(2)}, u32[]{:S(2)}) collective-permute-start(f32[3,16,2048]{2,1,0:T(8,128)S(1)} %first_units.1.first_ref.own_first_ref), channel_id=1, source_target_pairs={{0,1},{1,0},{2,3},{3,2},{4,5},{5,4},{6,7},{7,6},{8,9},{9,8},{10,11... | collective-permute-start | bytes 1179656 | tf_op jit(solution)/shard_map/ppermute | solution.py:390
  33.4 3.9 %collective-permute-start.2 = (f32[64,128]{1,0:T(8,128)S(1)}, f32[64,128]{1,0:T(8,128)S(1)}, u32[]{:S(2)}, u32[]{:S(2)}) collective-permute-start(f32[64,128]{1,0:T(8,128)S(1)} %pad_maximum_fusion), channel_id=1, source_target_pairs={{0,4},{2,6},{4,0},{6,2},{8,12},{10,14},{12,8},{14,10},{16,20},{18,... | collective-permute-start | bytes 98312 | tf_op jit(solution)/shard_map/ppermute | solution.py:387
  34.7 25.5 %collective-permute-start.6 = (f32[2,16,2048]{2,1,0:T(8,128)S(1)}, f32[2,16,2048]{2,1,0:T(8,128)S(1)}, u32[]{:S(2)}, u32[]{:S(2)}) collective-permute-start(f32[2,16,2048]{2,1,0:T(8,128)S(1)} %get-tuple-element.9.own_ref), channel_id=1, source_target_pairs={{0,1},{1,0},{2,3},{3,2},{4,5},{5,4},{6,7},{7,6},{8,9},{9,8},{10,11... | collective-permute-start | bytes 786440 | tf_op jit(solution)/shard_map/ppermute | solution.py:397
  37.3 4.0 %collective-permute-start.3 = (f32[64,128]{1,0:T(8,128)S(1)}, f32[64,128]{1,0:T(8,128)S(1)}, u32[]{:S(2)}, u32[]{:S(2)}) collective-permute-start(f32[64,128]{1,0:T(8,128)S(1)} %fusion), channel_id=1, source_target_pairs={{0,8},{2,10},{4,12},{6,14},{8,0},{10,2},{12,4},{14,6},{16,24},{18,... | collective-permute-start | bytes 98312 | tf_op jit(solution)/shard_map/ppermute | solution.py:387
  41.3 4.8 %collective-permute-start.4 = (f32[64,128]{1,0:T(8,128)S(1)}, f32[64,128]{1,0:T(8,128)S(1)}, u32[]{:S(2)}, u32[]{:S(2)}) collective-permute-start(f32[64,128]{1,0:T(8,128)S(1)} %add.14), channel_id=1, source_target_pairs={{0,16},{2,18},{4,20},{6,22},{8,24},{10,26},{12,28},{14,30},{16,0},... | collective-permute-start | bytes 98312 | tf_op jit(solution)/shard_map/ppermute | solution.py:387
  46.1 1.2 %collective-permute-start.5 = (f32[64,128]{1,0:T(8,128)S(1)}, f32[64,128]{1,0:T(8,128)S(1)}, u32[]{:S(2)}, u32[]{:S(2)}) collective-permute-start(f32[64,128]{1,0:T(8,128)S(1)} %add.15.part_ref), channel_id=1, source_target_pairs={{0,2},{2,0},{4,6},{6,4},{8,10},{10,8},{12,14},{14,12},{16,18},{18,... | collective-permute-start | bytes 98312 | tf_op jit(solution)/shard_map/ppermute | solution.py:403

commit v6 on v5

--- a/solution.py
+++ b/solution.py
@@ -127,11 +127,22 @@
     return jnp.broadcast_to(row, (SUBS, row.shape[1]))
 
 
+def thirds(x):
+    parts = []
+    for _ in range(3):
+        parts.append(x.astype(jnp.bfloat16))
+        x = x - parts[-1].astype(jnp.float32)
+    return parts
+
+
 def left_factor(mat):
-    high = mat.astype(jnp.bfloat16)
-    low = (mat - high.astype(jnp.float32)).astype(jnp.bfloat16)
-    return jnp.concatenate(
-        [jnp.concatenate([high, high], axis=1), jnp.concatenate([low, jnp.zeros_like(low)], axis=1)], axis=0)
+    high, mid, low = thirds(mat)
+    zero = jnp.zeros_like(low)
+    return jnp.concatenate([
+        jnp.concatenate([high, high, high], axis=1),
+        jnp.concatenate([mid, mid, zero], axis=1),
+        jnp.concatenate([low, zero, zero], axis=1),
+    ], axis=0)
 
 
 def chain_kernel(order_ref, owner_ref, mask_ref, var_ref, tile_ref, part_ref, back_ref, val_ref,
@@ -290,7 +301,7 @@
     f32 = jnp.float32
     return pl.pallas_call(
         chain_kernel,
-        out_shape=pltpu.VMEM((2 * half, 2 * members), jnp.bfloat16),
+        out_shape=pltpu.VMEM((3 * half, 3 * members), jnp.bfloat16),
         in_specs=[SMEM] * 5 + [VMEM] * 3,
         out_specs=VMEM,
         scratch_shapes=[
@@ -309,11 +320,9 @@
 
 def apply_block(left, own, upper, lower):
     half = own.shape[0]
-    x = jnp.concatenate([own, upper, lower], axis=0)
-    x_high = x.astype(jnp.bfloat16)
-    x_low = (x - x_high.astype(jnp.float32)).astype(jnp.bfloat16)
-    y = jnp.dot(left, jnp.concatenate([x_high, x_low], axis=0), preferred_element_type=jnp.float32)
-    return own + (y[:half] + y[half:])
+    x = jnp.concatenate(thirds(jnp.concatenate([own, upper, lower], axis=0)), axis=0)
+    y = jnp.dot(left, x, preferred_element_type=jnp.float32)
+    return own + ((y[2 * half:] + y[half:2 * half]) + y[:half])
 
 
 def apply_main(mat_ref, own_first_ref, own_main_ref, first_ref, main_ref, out_hbm, new_ref, sem_out):

time: 61.3 us -> 61.6 us (level)
  no operation moved by 1% of the time
where the time goes in v6:
time: 61.6 us; the launch traced here: 61.4 us
  waiting for transfers between devices  31.7 us (51%)
  Pallas kernels  17.1 us (28%)
  starting transfers between devices  12.4 us (20%)
    ppermute x1, waiting for transfers between devices, body(): oth = lax.ppermute(own, 'mem', swap)  23.9 us
    pallas_call x1, Pallas kernels, chain(): pl.pallas_call(chain_kernel, out_shape=pltpu.VMEM((3 * half, 3 * members)...  11.4 us
    ppermute x4, waiting for transfers between devices, across(): return lax.ppermute(x, 'tile', [(i, i ^ step) for i in range(n_tile)])  6.67 us
    ppermute x4, starting transfers between devices, across(): return lax.ppermute(x, 'tile', [(i, i ^ step) for i in range(n_tile)])  5.72 us
    ppermute x1, starting transfers between devices, body(): main = lax.ppermute(own_main, 'mem', swap)  3.06 us
    pallas_call x1, Pallas kernels, gather_rows(): pl.pallas_call(gather_kernel, out_shape=(pltpu.VMEM((2 * half, batches *...  2.06 us
    ppermute x1, starting transfers between devices, body(): first = lax.ppermute(own_first, 'mem', swap)  1.95 us
    pallas_call x1, Pallas kernels, apply_matrix(): pl.pallas_call(apply_main, out_shape=state, in_specs=[VMEM] * 5, out_spec...  1.61 us
  transfers between devices with their start and end apart: 9, of which 6 were waited for; matrix products, arithmetic and copies ran while one was open for 0% of the time, Pallas kernels for 21%

profile of v6, /device:TPU:0, one launch (start us, length us, event | category | flops | bytes accessed | tf_op | source)
XLA Modules:
  0.0 61.4 jit_solution(6658317546360179129)
XLA Ops:
  0.0 1.0 %first_units.1.first_ref.own_first_ref = f32[3,16,2048]{2,1,0:T(8,128)S(1)} custom-call(f32[14,16,2048]{2,1,0:T(8,128)} %bitcast.5), custom_call_target="tpu_custom_call" | custom-call | tf_op jit(solution)/shard_map/first_units/pallas_call | solution.py:33
  1.0 0.0 copy-start
  1.0 0.0 copy-start.1
  1.0 0.0 copy-start.2
  1.0 0.0 copy-start.3
  1.1 0.0 copy-start.4
  1.1 2.1 %gather_rows.1 = (f32[32,256]{1,0:T(8,128)S(1)}, f32[9,16,2048]{2,1,0:T(8,128)S(1)}, f32[2,16,2048]{2,1,0:T(8,128)S(1)}) custom-call(s32[8,32]{1,0:T(8,128)} %site_hbm.1, s32[8]{0:T(128)} %owner_ref.1, s32[8]{0:T(128)} %order_ref.1, f32[14,16,2048]{2,1,0:T(8,128)} %bitcast.6, f32[3,16,2048]{2,1,0:T(8,128)S(1)} %first_units.1.first_ref.own_first_ref), custom_call_target="tpu_custom_call" | custom-call | tf_op jit(solution)/shard_map/gather_rows/pallas_call | solution.py:106
  3.1 3.1 %collective-permute-start.8 = (f32[9,16,2048]{2,1,0:T(8,128)S(1)}, f32[9,16,2048]{2,1,0:T(8,128)S(1)}, u32[]{:S(2)}, u32[]{:S(2)}) collective-permute-start(f32[9,16,2048]{2,1,0:T(8,128)S(1)} %get-tuple-element.10.own_main_ref), channel_id=1, source_target_pairs={{0,1},{1,0},{2,3},{3,2},{4,5},{5,4},{6,7},{7,6},{8,9},{9,8},{10,11... | collective-permute-start | bytes 3538952 | tf_op jit(solution)/shard_map/ppermute | solution.py:405
  6.2 0.0 collective-permute-start
  6.2 1.2 %collective-permute-done = f32[32,256]{1,0:T(8,128)S(1)} collective-permute-done((f32[32,256]{1,0:T(8,128)S(1)}, f32[32,256]{1,0:T(8,128)S(1)}, u32[]{:S(2)}, u32[]{:S(2)}) %collective-permute-start) | collective-permute-done | bytes 32800 | tf_op jit(solution)/shard_map/ppermute | solution.py:396
  7.4 0.1 collective-permute-start.1
  7.6 1.9 %collective-permute-start.7 = (f32[3,16,2048]{2,1,0:T(8,128)S(1)}, f32[3,16,2048]{2,1,0:T(8,128)S(1)}, u32[]{:S(2)}, u32[]{:S(2)}) collective-permute-start(f32[3,16,2048]{2,1,0:T(8,128)S(1)} %first_units.1.first_ref.own_first_ref), channel_id=1, source_target_pairs={{0,1},{1,0},{2,3},{3,2},{4,5},{5,4},{6,7},{7,6},{8,9},{9,8},{10,11... | collective-permute-start | bytes 1179656 | tf_op jit(solution)/shard_map/ppermute | solution.py:399
  9.5 23.9 %collective-permute-done.1 = f32[32,128]{1,0:T(8,128)S(1)} collective-permute-done((f32[32,128]{1,0:T(8,128)S(1)}, f32[32,128]{1,0:T(8,128)S(1)}, u32[]{:S(2)}, u32[]{:S(2)}) %collective-permute-start.1) | collective-permute-done | bytes 16416 | tf_op jit(solution)/shard_map/ppermute | solution.py:404
  33.4 1.3 %collective-permute-start.2 = (f32[64,128]{1,0:T(8,128)S(1)}, f32[64,128]{1,0:T(8,128)S(1)}, u32[]{:S(2)}, u32[]{:S(2)}) collective-permute-start(f32[64,128]{1,0:T(8,128)S(1)} %pad_maximum_fusion), channel_id=1, source_target_pairs={{0,4},{2,6},{4,0},{6,2},{8,12},{10,14},{12,8},{14,10},{16,20},{18,... | collective-permute-start | bytes 98312 | tf_op jit(solution)/shard_map/ppermute | solution.py:396
  34.7 1.5 %collective-permute-start.6 = (f32[2,16,2048]{2,1,0:T(8,128)S(1)}, f32[2,16,2048]{2,1,0:T(8,128)S(1)}, u32[]{:S(2)}, u32[]{:S(2)}) collective-permute-start(f32[2,16,2048]{2,1,0:T(8,128)S(1)} %get-tuple-element.9.own_ref), channel_id=1, source_target_pairs={{0,1},{1,0},{2,3},{3,2},{4,5},{5,4},{6,7},{7,6},{8,9},{9,8},{10,11... | collective-permute-start | bytes 786440 | tf_op jit(solution)/shard_map/ppermute | solution.py:406
  36.2 1.1 %collective-permute-done.2 = f32[64,128]{1,0:T(8,128)S(1)} collective-permute-done((f32[64,128]{1,0:T(8,128)S(1)}, f32[64,128]{1,0:T(8,128)S(1)}, u32[]{:S(2)}, u32[]{:S(2)}) %collective-permute-start.2) | collective-permute-done | bytes 32800 | tf_op jit(solution)/shard_map/ppermute | solution.py:396
  37.3 2.1 %collective-permute-start.3 = (f32[64,128]{1,0:T(8,128)S(1)}, f32[64,128]{1,0:T(8,128)S(1)}, u32[]{:S(2)}, u32[]{:S(2)}) collective-permute-start(f32[64,128]{1,0:T(8,128)S(1)} %fusion), channel_id=1, source_target_pairs={{0,8},{2,10},{4,12},{6,14},{8,0},{10,2},{12,4},{14,6},{16,24},{18,... | collective-permute-start | bytes 98312 | tf_op jit(solution)/shard_map/ppermute | solution.py:396
  39.4 1.9 %collective-permute-done.3 = f32[64,128]{1,0:T(8,128)S(1)} collective-permute-done((f32[64,128]{1,0:T(8,128)S(1)}, f32[64,128]{1,0:T(8,128)S(1)}, u32[]{:S(2)}, u32[]{:S(2)}) %collective-permute-start.3) | collective-permute-done | bytes 32800 | tf_op jit(solution)/shard_map/ppermute | solution.py:396
  41.3 2.3 %collective-permute-start.4 = (f32[64,128]{1,0:T(8,128)S(1)}, f32[64,128]{1,0:T(8,128)S(1)}, u32[]{:S(2)}, u32[]{:S(2)}) collective-permute-start(f32[64,128]{1,0:T(8,128)S(1)} %add.14), channel_id=1, source_target_pairs={{0,16},{2,18},{4,20},{6,22},{8,24},{10,26},{12,28},{14,30},{16,0},... | collective-permute-start | bytes 98312 | tf_op jit(solution)/shard_map/ppermute | solution.py:396
  43.6 2.5 %collective-permute-done.4 = f32[64,128]{1,0:T(8,128)S(1)} collective-permute-done((f32[64,128]{1,0:T(8,128)S(1)}, f32[64,128]{1,0:T(8,128)S(1)}, u32[]{:S(2)}, u32[]{:S(2)}) %collective-permute-start.4) | collective-permute-done | bytes 32800 | tf_op jit(solution)/shard_map/ppermute | solution.py:396
  46.1 0.0 collective-permute-start.5
  46.1 1.2 %collective-permute-done.5.back_ref = f32[64,128]{1,0:T(8,128)S(1)} collective-permute-done((f32[64,128]{1,0:T(8,128)S(1)}, f32[64,128]{1,0:T(8,128)S(1)}, u32[]{:S(2)}, u32[]{:S(2)}) %collective-permute-start.5) | collective-permute-done | bytes 32800 | tf_op jit(solution)/shard_map/ppermute | solution.py:412
  47.3 0.0 copy-done
  47.3 0.0 copy-done.1
  47.3 0.0 copy-done.2
  47.3 0.0 copy-done.3
  47.3 0.0 copy-done.4
  47.3 11.4 %chain.1.mat_ref = bf16[96,192]{1,0:T(8,128)(2,1)S(1)} custom-call(s32[8]{0:T(128)S(1)} %copy-done.3, s32[8]{0:T(128)S(1)} %copy-done.4, s32[8,16]{1,0:T(8,128)S(1)} %copy-done, f32[8,32]{1,0:T(8,128)S(1)} %copy-done.1, s32[1]{0:T(128)} %bitcast.tile_ref, f32[64,128]{1,0:T(8,128)S(1)} %add.15.part_ref, f32[64,128]{1,0:T(8,128)S(1)} %collective-permute-done.5.back_ref, ...), custom_call_target="tpu_custom_call" | custom-call | tf_op jit(solution)/shard_map/chain/pallas_call | solution.py:302
  58.8 0.0 collective-permute-done.7.first_ref
  58.8 0.0 collective-permute-done.8.main_ref
  58.8 1.6 %apply_main.1.prev_hbm = f32[7,32,2048]{2,1,0:T(8,128)} custom-call(bf16[96,192]{1,0:T(8,128)(2,1)S(1)} %chain.1.mat_ref, f32[3,16,2048]{2,1,0:T(8,128)S(1)} %first_units.1.first_ref.own_first_ref, f32[9,16,2048]{2,1,0:T(8,128)S(1)} %get-tuple-element.10.own_main_ref, f32[3,16,2048]{2,1,0:T(8,128)S(1)} %collective-permute-done.7.first_ref, ...), custom_call_target="tpu_custom_call" | custom-call | tf_op jit(solution)/shard_map/apply_main/pallas_call | solution.py:365
  60.4 0.0 collective-permute-done.6.last_ref
  60.4 1.0 %apply_last.1 = f32[7,32,2048]{2,1,0:T(8,128)} custom-call(bf16[96,192]{1,0:T(8,128)(2,1)S(1)} %chain.1.mat_ref, f32[2,16,2048]{2,1,0:T(8,128)S(1)} %get-tuple-element.9.own_ref, f32[2,16,2048]{2,1,0:T(8,128)S(1)} %collective-permute-done.6.last_ref, f32[7,32,2048]{2,1,0:T(8,128)} %apply_main.1.prev_hbm), custom_call_target="tpu_custom_call", output_to_operand_aliasing={{}: (3, {})} | custom-call | tf_op jit(solution)/shard_map/apply_last/pallas_call | solution.py:374
  (6 shorter events, 0.0 us)
Async XLA Ops:
  1.0 46.3 %copy-start = (s32[8,16]{1,0:T(8,128)S(1)}, s32[8,16]{1,0:T(8,128)}, u32[]{:S(2)}) copy-start(s32[8,16]{1,0:T(8,128)} %mask_ref.1) | copy-start | bytes 1540
  1.0 46.3 %copy-start.1 = (f32[8,32]{1,0:T(8,128)S(1)}, f32[8,32]{1,0:T(8,128)}, u32[]{:S(2)}) copy-start(f32[8,32]{1,0:T(8,128)} %var_ref.1) | copy-start | bytes 3076
  1.0 46.3 %copy-start.2 = (f32[8,32]{1,0:T(8,128)S(1)}, f32[8,32]{1,0:T(8,128)}, u32[]{:S(2)}) copy-start(f32[8,32]{1,0:T(8,128)} %val_ref.1) | copy-start | bytes 3076
  1.0 46.3 %copy-start.3 = (s32[8]{0:T(128)S(1)}, s32[8]{0:T(128)}, u32[]{:S(2)}) copy-start(s32[8]{0:T(128)} %order_ref.1) | copy-start | bytes 100
  1.1 46.3 %copy-start.4 = (s32[8]{0:T(128)S(1)}, s32[8]{0:T(128)}, u32[]{:S(2)}) copy-start(s32[8]{0:T(128)} %owner_ref.1) | copy-start | bytes 100
  3.1 55.6 %collective-permute-start.8 = (f32[9,16,2048]{2,1,0:T(8,128)S(1)}, f32[9,16,2048]{2,1,0:T(8,128)S(1)}, u32[]{:S(2)}, u32[]{:S(2)}) collective-permute-start(f32[9,16,2048]{2,1,0:T(8,128)S(1)} %get-tuple-element.10.own_main_ref), channel_id=1, source_target_pairs={{0,1},{1,0},{2,3},{3,2},{4,5},{5,4},{6,7},{7,6},{8,9},{9,8},{10,11... | collective-permute-start | bytes 3538952 | tf_op jit(solution)/shard_map/ppermute | solution.py:405
  6.2 1.2 %collective-permute-start = (f32[32,256]{1,0:T(8,128)S(1)}, f32[32,256]{1,0:T(8,128)S(1)}, u32[]{:S(2)}, u32[]{:S(2)}) collective-permute-start(f32[32,256]{1,0:T(8,128)S(1)} %get-tuple-element.8), channel_id=1, source_target_pairs={{0,2},{2,0},{4,6},{6,4},{8,10},{10,8},{12,14},{14,12},{16,18},{18,... | collective-permute-start | bytes 98312 | tf_op jit(solution)/shard_map/ppermute | solution.py:396
  7.4 25.9 %collective-permute-start.1 = (f32[32,128]{1,0:T(8,128)S(1)}, f32[32,128]{1,0:T(8,128)S(1)}, u32[]{:S(2)}, u32[]{:S(2)}) collective-permute-start(f32[32,128]{1,0:T(8,128)S(1)} %slice_select_fusion), channel_id=1, source_target_pairs={{0,1},{1,0},{2,3},{3,2},{4,5},{5,4},{6,7},{7,6},{8,9},{9,8},{10,11... | collective-permute-start | bytes 49160 | tf_op jit(solution)/shard_map/ppermute | solution.py:404
  7.6 51.2 %collective-permute-start.7 = (f32[3,16,2048]{2,1,0:T(8,128)S(1)}, f32[3,16,2048]{2,1,0:T(8,128)S(1)}, u32[]{:S(2)}, u32[]{:S(2)}) collective-permute-start(f32[3,16,2048]{2,1,0:T(8,128)S(1)} %first_units.1.first_ref.own_first_ref), channel_id=1, source_target_pairs={{0,1},{1,0},{2,3},{3,2},{4,5},{5,4},{6,7},{7,6},{8,9},{9,8},{10,11... | collective-permute-start | bytes 1179656 | tf_op jit(solution)/shard_map/ppermute | solution.py:399
  33.4 3.9 %collective-permute-start.2 = (f32[64,128]{1,0:T(8,128)S(1)}, f32[64,128]{1,0:T(8,128)S(1)}, u32[]{:S(2)}, u32[]{:S(2)}) collective-permute-start(f32[64,128]{1,0:T(8,128)S(1)} %pad_maximum_fusion), channel_id=1, source_target_pairs={{0,4},{2,6},{4,0},{6,2},{8,12},{10,14},{12,8},{14,10},{16,20},{18,... | collective-permute-start | bytes 98312 | tf_op jit(solution)/shard_map/ppermute | solution.py:396
  34.7 25.7 %collective-permute-start.6 = (f32[2,16,2048]{2,1,0:T(8,128)S(1)}, f32[2,16,2048]{2,1,0:T(8,128)S(1)}, u32[]{:S(2)}, u32[]{:S(2)}) collective-permute-start(f32[2,16,2048]{2,1,0:T(8,128)S(1)} %get-tuple-element.9.own_ref), channel_id=1, source_target_pairs={{0,1},{1,0},{2,3},{3,2},{4,5},{5,4},{6,7},{7,6},{8,9},{9,8},{10,11... | collective-permute-start | bytes 786440 | tf_op jit(solution)/shard_map/ppermute | solution.py:406
  37.3 4.0 %collective-permute-start.3 = (f32[64,128]{1,0:T(8,128)S(1)}, f32[64,128]{1,0:T(8,128)S(1)}, u32[]{:S(2)}, u32[]{:S(2)}) collective-permute-start(f32[64,128]{1,0:T(8,128)S(1)} %fusion), channel_id=1, source_target_pairs={{0,8},{2,10},{4,12},{6,14},{8,0},{10,2},{12,4},{14,6},{16,24},{18,... | collective-permute-start | bytes 98312 | tf_op jit(solution)/shard_map/ppermute | solution.py:396
  41.3 4.8 %collective-permute-start.4 = (f32[64,128]{1,0:T(8,128)S(1)}, f32[64,128]{1,0:T(8,128)S(1)}, u32[]{:S(2)}, u32[]{:S(2)}) collective-permute-start(f32[64,128]{1,0:T(8,128)S(1)} %add.14), channel_id=1, source_target_pairs={{0,16},{2,18},{4,20},{6,22},{8,24},{10,26},{12,28},{14,30},{16,0},... | collective-permute-start | bytes 98312 | tf_op jit(solution)/shard_map/ppermute | solution.py:396
  46.1 1.2 %collective-permute-start.5 = (f32[64,128]{1,0:T(8,128)S(1)}, f32[64,128]{1,0:T(8,128)S(1)}, u32[]{:S(2)}, u32[]{:S(2)}) collective-permute-start(f32[64,128]{1,0:T(8,128)S(1)} %add.15.part_ref), channel_id=1, source_target_pairs={{0,2},{2,0},{4,6},{6,4},{8,10},{10,8},{12,14},{14,12},{16,18},{18,... | collective-permute-start | bytes 98312 | tf_op jit(solution)/shard_map/ppermute | solution.py:412
